TPU v7x, 128 devices: a whole 4x4x4 slice. The times are simulated.
128 devices in a mesh: feat: 32 (over z, y, core), cls: 4 (over x).
Axes of the slice: x: 4, y: 4, z: 4, core: 2. Of those that a mesh axis runs over, the one named last changes fastest.
Arguments:
- inputs: bfloat16 [2, 1024, 360], P(None, 'feat'), may hold values from -6 to 6
- projection: bfloat16 [360, 65536], P(None, 'feat'), may hold values from -0.3125 to 0.3125
- offsets: int32 [65536], P('feat'), may hold values from 0 to 65520
- labels: int32 [2, 1024], replicated, may hold values from 0 to 4999
- weights: float32 [65536, 5000], P('feat', 'cls'), may hold values from -6 to 6
Outputs:
- updated_weights: float32 [65536, 5000], P('feat', 'cls')
- losses: float32 [2], replicated
All inputs are finite; a program needn't handle non-finite values.
Results may differ from a plain program's by a relative error of at most 0.00061.
Values may be sent and summed in bfloat16 or wider, within the bound.
A program may use at most 128 MiB of HBM per device.

v0:
```python
import math

import jax
import jax.numpy as jnp
from jax import lax
from jax.sharding import PartitionSpec as P

NFEAT = 65536
NCLS = 5000
PANELS = 2


learning_rate = 10.0


def per_device(inputs, projection, offsets, labels, weights):
    phase = offsets.astype(jnp.float32) * (2.0 * math.pi / 65521.0) - math.pi
    class_count = weights.shape[1]
    first_class = lax.axis_index("cls") * class_count
    classes = jnp.arange(class_count, dtype=jnp.int32) + first_class
    feature_scale = math.sqrt(2.0 / NFEAT)
    losses = []
    for panel_index in range(PANELS):
        angles = (
            jnp.dot(
                lax.all_gather(inputs[panel_index], "feat", axis=0, tiled=True),
                projection,
                preferred_element_type=jnp.float32,
            )
            + phase
        )
        features = (feature_scale * jnp.cos(angles)).astype(jnp.bfloat16)
        narrow = weights.astype(jnp.bfloat16)
        panel_labels = labels[panel_index]
        scores = lax.psum(jnp.dot(features, narrow, preferred_element_type=jnp.float32), "feat")
        is_target = panel_labels[:, None] == classes[None, :]
        target = lax.psum(jnp.sum(jnp.where(is_target, scores, 0.0), axis=1), "cls")
        margin = jnp.where(is_target, 0.0, jnp.maximum(0.0, 1.0 + scores - target[:, None]))
        slope = 2.0 * margin / (NCLS - 1)
        others, row_loss = lax.psum(
            (jnp.sum(slope, axis=1), jnp.sum(margin * margin, axis=1) / (NCLS - 1)), "cls"
        )
        step_grad = jnp.where(is_target, -others[:, None], slope).astype(jnp.bfloat16)
        gradient = lax.dot_general(
            features, step_grad, (((0,), (0,)), ((), ())), preferred_element_type=jnp.float32
        )
        loss = jnp.sum(row_loss)
        weights = weights - learning_rate * gradient
        losses.append(loss)
    return (weights, jnp.stack(losses))


def solution(mesh):
    return jax.shard_map(
        per_device,
        mesh=mesh,
        in_specs=(P(None, "feat", None), P(None, "feat"), P("feat"), P(), P("feat", "cls")),
        out_specs=(P("feat", "cls"), P()),
        check_vma=False,
    )
```

profile of v0, /device:TPU:1, one launch (start us, length us, event | category | flops | bytes accessed | tf_op | source)
XLA Modules:
  0.0 398.8 jit_solution(3330044593510233034)
XLA Ops:
  7.2 0.0 copy-start
  7.2 0.0 all-reduce.4.cloned.1.call-start
  7.2 0.8 multiply_add_fusion
  8.0 0.8 fusion.22
  8.8 27.7 %all-gather = bf16[1,1024,360]{2,1,0:T(8,128)(2,1)S(1)} all-gather(bf16[1,32,360]{2,1,0:T(8,128)(2,1)S(1)} %get-tuple-element.10), channel_id=2, replica_groups=mesh['feat'=32,'cls'=4] {'feat'}, dimensions={1}, use_global_device_ids=true | all-gather | bytes 760320 | tf_op jit(solution)/shard_map/all_gather | solution.py:26
  36.5 0.0 copy-done
  36.5 0.0 copy-start.2
  36.5 30.4 %multiply_convert_fusion.1 = bf16[1024,2048]{1,0:T(8,128)(2,1)S(1)} fusion(bf16[360,2048]{1,0:T(8,128)(2,1)S(1)} %copy-done, f32[2048]{0:T(1024)S(1)} %multiply_add_fusion, bf16[1,1024,360]{2,1,0:T(8,128)(2,1)S(1)} %all-gather), kind=kOutput, calls=%fused_computation.3 | convolution fusion | flops 1516240896 | bytes 6414336 | tf_op jit(solution)/shard_map/dot_general | solution.py:25
  66.9 0.0 copy-start.4
  67.0 2.0 copy-done.4
  68.9 0.0 copy-done.2
  68.9 7.4 %fusion.6 = f32[1024,1250]{0,1:T(8,128)} fusion(bf16[1024,2048]{1,0:T(8,128)(2,1)S(1)} %multiply_convert_fusion.1, f32[2048,1250]{0,1:T(8,128)S(1)} %copy-done.2), kind=kOutput, calls=%fused_computation.18 | convolution fusion | flops 5245440000 | bytes 19554304 | tf_op jit(solution)/shard_map/dot_general | solution.py:35
  76.4 0.0 copy-start.1
  76.4 0.0 all-reduce.4.cloned.1.call-update
  76.4 0.0 all-reduce.6.cloned.1.call-start
  76.4 24.4 %all-gather.1 = bf16[1,1024,360]{2,1,0:T(8,128)(2,1)S(1)} all-gather(bf16[1,32,360]{2,1,0:T(8,128)(2,1)S(1)} %get-tuple-element.9), channel_id=3, replica_groups=mesh['feat'=32,'cls'=4] {'feat'}, dimensions={1}, use_global_device_ids=true | all-gather | bytes 760320 | tf_op jit(solution)/shard_map/all_gather | solution.py:26
  100.8 0.0 copy-done.1
  100.8 31.3 %multiply_convert_fusion = bf16[1024,2048]{1,0:T(8,128)(2,1)} fusion(bf16[360,2048]{1,0:T(8,128)(2,1)S(1)} %copy-done, f32[2048]{0:T(1024)S(1)} %multiply_add_fusion, bf16[1,1024,360]{2,1,0:T(8,128)(2,1)S(1)} %all-gather.1), kind=kOutput, calls=%fused_computation.2 | convolution fusion | flops 1516240896 | bytes 6414336 | tf_op jit(solution)/shard_map/dot_general | solution.py:25
  132.1 57.8 %all-reduce.4.cloned.1.call-done = f32[1024,1250]{0,1:T(8,128)} async-done(((f32[1024,1250]{0,1:T(8,128)}), f32[1024,1250]{0,1:T(8,128)}) %all-reduce.4.cloned.1.call-update) | async-done | bytes 5120016 | tf_op jit(solution)/shard_map/psum | solution.py:35
  189.9 3.0 fusion
  192.9 8.4 %psum.57 = f32[1024]{0:T(1024)S(1)} all-reduce(f32[1024]{0:T(1024)S(1)} %fusion), channel_id=1, replica_groups=mesh['feat'=32,'cls'=4] {'cls'}, use_global_device_ids=true, to_apply=%region_2.3 | all-reduce | flops 1024 | bytes 8192 | tf_op jit(solution)/shard_map/psum | solution.py:37
  201.4 3.6 multiply_reduce_fusion.1
  204.9 6.0 %psum.58 = f32[1024]{0:T(1024)S(1)} all-reduce(f32[1024]{0:T(1024)S(1)} %get-tuple-element.3), channel_id=1, replica_groups=mesh['feat'=32,'cls'=4] {'cls'}, use_global_device_ids=true, to_apply=%region_4.5 | all-reduce | flops 1024 | bytes 8192 | tf_op jit(solution)/shard_map/psum | solution.py:40
  210.9 0.0 copy-start.3
  210.9 11.5 %multiply_subtract_fusion.1 = f32[2048,1250]{0,1:T(8,128)S(1)} fusion(f32[2048,1250]{0,1:T(8,128)} %param.9, bf16[1024,2048]{1,0:T(8,128)(2,1)} %copy-done.4, bf16[1024]{0:T(1024)(128)(2,1)S(1)} %neg.8, s32[1024]{0:T(1024)S(1)} %bitcast.21, s32[1250]{0:T(1024)S(1)} %iota_add_fusion, f32[1024,1250]{0,1:T(8,128)} %all-reduce.4.cloned.1.call-done, ...), kind=kOutput, calls=%fused_computation.1 | convolution fusion | flops 5256960000 | bytes 29809544 | tf_op jit(solution)/shard_map/dot_general | solution.py:44
  222.4 0.0 copy-start.5
  222.4 4.0 %copy-done.5 = f32[2048,1250]{0,1:T(8,128)} copy-done((f32[2048,1250]{0,1:T(8,128)}, f32[2048,1250]{0,1:T(8,128)S(1)}, u32[]{:S(2)}) %copy-start.5) | copy-done | bytes 10240024
  226.4 0.0 copy-done.3
  226.4 7.5 %fusion.4 = f32[1024,1250]{0,1:T(8,128)} fusion(bf16[1024,2048]{1,0:T(8,128)(2,1)S(1)} %copy-done.3, f32[2048,1250]{0,1:T(8,128)S(1)} %multiply_subtract_fusion.1), kind=kOutput, calls=%fused_computation.16 | convolution fusion | flops 5245440000 | bytes 19554304 | tf_op jit(solution)/shard_map/dot_general | solution.py:35
  233.9 0.0 all-reduce.6.cloned.1.call-update
  233.9 115.9 %all-reduce.6.cloned.1.call-done = f32[1024,1250]{0,1:T(8,128)} async-done(((f32[1024,1250]{0,1:T(8,128)}), f32[1024,1250]{0,1:T(8,128)}) %all-reduce.6.cloned.1.call-update) | async-done | bytes 5120016 | tf_op jit(solution)/shard_map/psum | solution.py:35
  349.9 3.0 fusion.2
  352.9 8.4 %psum.60 = f32[1024]{0:T(1024)S(1)} all-reduce(f32[1024]{0:T(1024)S(1)} %fusion.2), channel_id=1, replica_groups=mesh['feat'=32,'cls'=4] {'cls'}, use_global_device_ids=true, to_apply=%region_7.8 | all-reduce | flops 1024 | bytes 8192 | tf_op jit(solution)/shard_map/psum | solution.py:37
  361.3 3.6 multiply_reduce_fusion
  364.9 10.8 %all-reduce = (f32[1024]{0:T(1024)S(1)}, f32[1024]{0:T(1024)S(1)}, f32[1024]{0:T(1024)S(1)}) all-reduce(f32[1024]{0:T(1024)S(1)} %get-tuple-element.5, f32[1024]{0:T(1024)S(1)} %broadcast_multiply_fusion, f32[1024]{0:T(1024)S(1)} %broadcast_multiply_fusion.1), channel_id=1, replica_groups=mesh['feat'=32,'cls'=4] {'cls'}, use_global_device_ids=true, to_apply=%region_9.10 | all-reduce | flops 3072 | bytes 24576 | tf_op jit(solution)/shard_map/psum | solution.py:40
  375.7 0.6 reduce_sum.77
  376.4 0.7 reduce_sum.79
  377.0 1.9 pad_maximum_fusion
  378.9 13.0 %multiply_subtract_fusion = f32[2048,1250]{0,1:T(8,128)} fusion(f32[2048,1250]{0,1:T(8,128)} %copy-done.5, bf16[1024,2048]{1,0:T(8,128)(2,1)} %multiply_convert_fusion, bf16[1024]{0:T(1024)(128)(2,1)S(1)} %neg.9, s32[1024]{0:T(1024)S(1)} %bitcast.18, s32[1250]{0:T(1024)S(1)} %iota_add_fusion, f32[1024,1250]{0,1:T(8,128)} %all-reduce.6.cloned.1.call-done, ...), kind=kOutput, calls=%fused_computation | convolution fusion | flops 5256960000 | bytes 29809544 | tf_op jit(solution)/shard_map/dot_general | solution.py:44
  (6 shorter events, 0.0 us)
Async XLA Ops:
  7.2 29.3 %copy-start = (bf16[360,2048]{1,0:T(8,128)(2,1)S(1)}, bf16[360,2048]{1,0:T(8,128)(2,1)}, u32[]{:S(2)}) copy-start(bf16[360,2048]{1,0:T(8,128)(2,1)} %param.6) | copy-start | bytes 4423684
  7.2 182.7 %all-reduce.4.cloned.1.call-start = ((), (), s32[]{:S(2)}) async-start(), calls=%async_computation | async-start | bytes 10289152 | tf_op jit(solution)/shard_map/psum | solution.py:35
  36.5 32.5 %copy-start.2 = (f32[2048,1250]{0,1:T(8,128)S(1)}, f32[2048,1250]{0,1:T(8,128)}, u32[]{:S(2)}) copy-start(f32[2048,1250]{0,1:T(8,128)} %param.9) | copy-start | bytes 30720004
  66.9 2.0 copy-start.4
  76.4 24.5 %copy-start.1 = (s32[2,1024]{1,0:T(2,128)S(1)}, s32[2,1024]{1,0:T(2,128)}, u32[]{:S(2)}) copy-start(s32[2,1024]{1,0:T(2,128)} %param.8) | copy-start | bytes 24580
  76.4 273.5 %all-reduce.6.cloned.1.call-start = ((), (), s32[]{:S(2)}) async-start(), calls=%async_computation.1 | async-start | bytes 10289152 | tf_op jit(solution)/shard_map/psum | solution.py:35
  210.9 15.5 %copy-start.3 = (bf16[1024,2048]{1,0:T(8,128)(2,1)S(1)}, bf16[1024,2048]{1,0:T(8,128)(2,1)}, u32[]{:S(2)}) copy-start(bf16[1024,2048]{1,0:T(8,128)(2,1)} %multiply_convert_fusion) | copy-start | bytes 12582916
  222.4 4.0 %copy-start.5 = (f32[2048,1250]{0,1:T(8,128)}, f32[2048,1250]{0,1:T(8,128)S(1)}, u32[]{:S(2)}) copy-start(f32[2048,1250]{0,1:T(8,128)S(1)} %multiply_subtract_fusion.1) | copy-start | bytes 30720004
Sparse Core Ops, SparseCore 0:
  76.5 113.3 all-reduce.3
  234.1 115.7 all-reduce.5
where the time goes:
time: 404 us; the launch traced here: 399 us
  waiting for transfers between devices  174 us (43%)
  matrix products  101 us (25%)
  blocking collectives  85.7 us (21%)
  other arithmetic  17.2 us (4%)
  between operations  14.2 us (4%)
  local copies, waits for them, and re-layouts  6.8 us (2%)
    psum x2, waiting for transfers between devices, per_device(): lax.psum(jnp.dot(features, narrow, preferred_element_type=jnp.float32), '...  174 us
    dot_general x2, matrix products, per_device(): jnp.dot(lax.all_gather(inputs[panel_index], 'feat', axis=0, tiled=True),...  61.7 us
    all_gather x2, blocking collectives, per_device(): lax.all_gather(inputs[panel_index], 'feat', axis=0, tiled=True)  52.1 us
    dot_general x2, matrix products, per_device(): lax.dot_general(features, step_grad, (((0,), (0,)), ((), ())), preferred_...  24.5 us
    psum x2, blocking collectives, per_device(): target = lax.psum(jnp.sum(jnp.where(is_target, scores, 0.0), axis=1), 'cls')  16.8 us
    psum x2, blocking collectives, per_device(): lax.psum((jnp.sum(slope, axis=1), jnp.sum(margin * margin, axis=1) / (NCL...  16.8 us
    dot_general x2, matrix products, per_device(): jnp.dot(features, narrow, preferred_element_type=jnp.float32)  14.9 us
  transfers between devices with their start and end apart: 2, of which 2 were waited for; matrix products, arithmetic and copies ran while one was open for 8% of the time, Pallas kernels for 0%

commit v1 on v0

v1 whole, which is shorter than its diff:
```python
import math

import jax
import jax.numpy as jnp
from jax import lax
from jax.experimental import pallas as pl
from jax.experimental.pallas import tpu as pltpu
from jax.sharding import PartitionSpec as P

DIN, DPAD = 360, 384
NFEAT = 65536
NCLS = 5000
FRAMES = 1024
FEATS = 2048
CLS = 1250
CPAD = 1280
GRAM = 256
RATE = 10.0
MESH = pl.DeviceIdType.MESH
BF, F32 = jnp.bfloat16, jnp.float32
SINE = (6.2831851595779975, -41.34165492085313, 81.60099762206104, -76.54964291002278, 39.53570242669577)


def m4(v):
    return lax.rem(v, 4)


def step_kernel(
    inp, proj, off, lab, w_hbm,
    f1_hbm, g_hbm, wp_hbm,
    xb, pb, wf, wn, fb, ows, owk, ps, pr, psk, prk,
    s1_0, s1_1, r1_0, r1_1, s2_0, s2_1, r2_0, r2_1, own_0, own_1,
    so, sk, kg, tg, ox, lt, gb, ssem, rsem, lsem,
):
    feat, x = lax.axis_index("feat"), lax.axis_index("cls")
    c = lax.rem(feat, 2)
    y = m4(feat // 2)
    z = feat // 8
    p1 = y * (1 - c) + z * c
    p2 = z * (1 - c) + y * c

    def at(a, b):
        return ((b * (1 - c) + a * c) * 8 + (a * (1 - c) + b * c) * 2 + c, x)

    right1, left1 = at(m4(p1 + 1), p2), at(m4(p1 + 3), p2)
    right2, left2 = at(p1, m4(p2 + 1)), at(p1, m4(p2 + 3))
    partner = (feat + 1 - 2 * c, x)
    others_x = [(feat, m4(x + j)) for j in (1, 2, 3)]

    drain = []

    def rc(src, dst, i, dev):
        return pltpu.make_async_remote_copy(
            src_ref=src, dst_ref=dst, send_sem=ssem.at[i], recv_sem=rsem.at[i], device_id=dev, device_id_type=MESH
        )

    def send(ends, i, dev):
        rc(*ends(), i, dev).start()
        drain.append(lambda: rc(*ends(), i, dev).wait_send())

    def recv(region, i):
        rc(region, region, i, partner).wait_recv()

    counter = [0]

    def sems(n):
        counter[0] += n
        return counter[0] - n

    def rows_at(cc, b1, b2=0, extra=0, size=128):
        start = cc * 512 + b1 * 128 + b2 * 32 + extra
        return pl.ds(pl.multiple_of(start, min(size, 128)), size)

    w_in = [pltpu.make_async_copy(w_hbm.at[pl.ds(t * 256, 256)], wf.at[pl.ds(t * 256, 256)], lsem.at[t]) for t in range(8)]
    proj_in = pltpu.make_async_copy(proj, pb.at[pl.ds(0, DIN)], lsem.at[8])
    proj_in.start()
    for cp in w_in:
        cp.start()

    own = lambda: rows_at(c, p1, p2, 0, 32)
    for p in range(2):
        xb[p, own(), :] = jnp.zeros((32, DPAD), BF)
        xb[p, own(), 0:DIN] = inp[p]

    barrier = pltpu.get_barrier_semaphore()
    for dev in [right1, left1, right2, left2, partner] + others_x:
        pl.semaphore_signal(barrier, inc=1, device_id=dev, device_id_type=MESH)
    pl.semaphore_wait(barrier, 8)

    class Gather:
        def __init__(self, buf):
            self.buf = buf
            self.base = sems(12)

        def put(self, rows, i, dev):
            send(lambda: (self.buf().at[rows()], self.buf().at[rows()]), self.base + i, dev)

        def take(self, rows, i):
            recv(self.buf().at[rows()], self.base + i)

        def step0(self):
            self.put(own, 0, right2)
            self.put(own, 1, left2)

        def step1(self):
            self.take(lambda: rows_at(c, p1, m4(p2 + 3), 0, 32), 0)
            self.put(lambda: rows_at(c, p1, m4(p2 + 3), 0, 16), 2, right2)
            self.take(lambda: rows_at(c, p1, m4(p2 + 1), 0, 32), 1)
            self.put(lambda: rows_at(c, p1, m4(p2 + 1), 16, 16), 3, left2)

        def step2(self):
            self.take(lambda: rows_at(c, p1, m4(p2 + 2), 0, 16), 2)
            self.take(lambda: rows_at(c, p1, m4(p2 + 2), 16, 16), 3)
            blk = lambda: rows_at(c, p1)
            self.put(blk, 4, right1)
            self.put(blk, 5, left1)
            self.put(blk, 8, partner)

        def step3(self):
            self.take(lambda: rows_at(c, m4(p1 + 3)), 4)
            self.put(lambda: rows_at(c, m4(p1 + 3), 0, 0, 64), 6, right1)
            self.put(lambda: rows_at(c, m4(p1 + 3)), 9, partner)
            self.take(lambda: rows_at(c, m4(p1 + 1)), 5)
            self.put(lambda: rows_at(c, m4(p1 + 1), 0, 64, 64), 7, left1)
            self.put(lambda: rows_at(c, m4(p1 + 1)), 10, partner)

        def step4(self):
            self.take(lambda: rows_at(c, m4(p1 + 2), 0, 0, 64), 6)
            self.take(lambda: rows_at(c, m4(p1 + 2), 0, 64, 64), 7)
            self.put(lambda: rows_at(c, m4(p1 + 2)), 11, partner)

        def step5(self):
            for i, d in enumerate((0, 3, 1, 2)):
                self.take(lambda: rows_at(1 - c, m4(p2 + d)), 8 + i)

    gx = [Gather(lambda p=p: xb.at[p]) for p in range(2)]
    gg = [Gather(lambda p=p: gb.at[p]) for p in range(2)]

    gx[0].step0()
    gx[1].step0()

    pb[DIN:DPAD, :] = jnp.zeros((DPAD - DIN, FEATS), BF)
    turns = off[...].astype(F32) * F32(1.0 / 65521.0)
    lab_col = pl.multiple_of((feat // 4) * 128, 128)
    for p in range(2):
        row = lab[pl.ds(p, 1), pl.ds(lab_col, 128)].astype(F32)
        lt[p] = jnp.broadcast_to(row, (128, 128)).T
    gx[0].step1()
    gx[1].step1()
    wn[:, 1152:CPAD] = jnp.zeros((FEATS, CPAD - 1152), BF)

    def narrow(t):
        w_in[t].wait()
        wn[pl.ds(t * 256, 256), 0:CLS] = wf[pl.ds(t * 256, 256), :].astype(BF)

    narrow(0)
    gx[0].step2()
    gx[1].step2()
    narrow(1)
    narrow(2)
    gx[0].step3()
    narrow(3)
    narrow(4)
    gx[0].step4()
    gx[1].step3()
    narrow(5)
    narrow(6)
    narrow(7)
    proj_in.wait()
    gx[0].step5()

    scale = math.sqrt(2.0 / NFEAT)
    coef = [F32(v * scale) for v in SINE]

    def features(p, rows):
        acc = jnp.dot(xb[p, rows, :], pb[...], preferred_element_type=F32)
        u = acc * F32(1.0 / (2.0 * math.pi)) + turns
        q = jnp.abs(u - jnp.round(u)) - 0.25
        q2 = q * q
        r = coef[4]
        for v in coef[3::-1]:
            r = r * q2 + v
        fb[p, rows, :] = (r * q).astype(BF)

    def scores(p, rows):
        return jnp.dot(fb[p, rows, :], wn[...], preferred_element_type=F32)

    def gram(rows):
        quarter = pl.ds(pl.multiple_of(x * GRAM, GRAM), GRAM)
        return lax.dot_general(
            fb[1, rows, :], fb[0, quarter, :], (((1,), (1,)), ((), ())), preferred_element_type=F32
        )

    S1, R1, S2, R2, OWN = (s1_0, s1_1), (r1_0, r1_1), (s2_0, s2_1), (r2_0, r2_1), (own_0, own_1)
    pair_sem = sems(12)
    ring_sem = [sems(8), sems(8)]
    tg_sem, ox_sem, kg_sem = [sems(3), sems(3)], [sems(3), sems(3)], sems(3)

    def pair_recv(p, k):
        recv(pr.at[4 * p + k], pair_sem + 4 * p + k)
        if p:
            recv(prk.at[k], pair_sem + 8 + k)

    def combine(p, k, put, lo, hi):
        def body(i, _):
            rows = pl.ds(pl.multiple_of(i * 32, 32), 32)
            put(rows, slice(0, CPAD), ows[k, rows, :] + pr[4 * p + k, rows, :].astype(F32))
            if p:
                put(rows, slice(CPAD, CPAD + GRAM), owk[k, rows, :] + prk[k, rows, :].astype(F32))
            return 0

        lax.fori_loop(lo, hi, body, 0)

    def reduce0(p):
        pair_recv(p, 0)
        s, r, i = S1[p], R1[p], ring_sem[p]

        def put(rows, cols, v):
            s[0, rows, cols] = v.astype(BF)

        combine(p, 0, put, 0, 4)
        send(lambda: (s.at[0, pl.ds(0, 64)], r.at[pl.ds(0, 64)]), i, right1)
        send(lambda: (s.at[0, pl.ds(64, 64)], r.at[pl.ds(64, 64)]), i + 1, left1)

    def reduce1(p):
        pair_recv(p, 1)
        s, r, i = S1[p], R1[p], ring_sem[p]
        recv(r.at[pl.ds(0, 64)], i)

        def put_in(rows, cols, v):
            s[1, rows, cols] = (v + r[rows, cols].astype(F32)).astype(BF)

        def put(rows, cols, v):
            s[1, rows, cols] = v.astype(BF)

        combine(p, 1, put_in, 0, 2)
        combine(p, 1, put, 2, 4)
        send(lambda: (s.at[1], r.at[pl.ds(128, 128)]), i + 2, right1)

    def reduce2(p):
        pair_recv(p, 2)
        s, r, i = S1[p], R1[p], ring_sem[p]
        recv(r.at[pl.ds(64, 64)], i + 1)

        def put_in(rows, cols, v):
            s[2, rows, cols] = (v + r[rows, cols].astype(F32)).astype(BF)

        def put(rows, cols, v):
            s[2, rows, cols] = v.astype(BF)

        combine(p, 2, put, 0, 2)
        combine(p, 2, put_in, 2, 4)
        send(lambda: (s.at[2], r.at[pl.ds(256, 128)]), i + 3, left1)

    def sub(d, extra=0, size=32):
        return pl.ds(pl.multiple_of(m4(p2 + d) * 32 + extra, 16), size)

    def reduce3(p):
        pair_recv(p, 3)
        r, i, o = R1[p], ring_sem[p], OWN[p]
        recv(r.at[pl.ds(128, 128)], i + 2)
        recv(r.at[pl.ds(256, 128)], i + 3)

        def put(rows, cols, v):
            a = pl.ds(pl.multiple_of(rows.start + 128, 32), 32)
            b = pl.ds(pl.multiple_of(rows.start + 256, 32), 32)
            o[rows, cols] = v + r[a, cols].astype(F32) + r[b, cols].astype(F32)

        combine(p, 3, put, 0, 4)
        s, r = S2[p], R2[p]
        s[pl.ds(0, 32), :] = o[sub(2), :].astype(BF)
        send(lambda: (s.at[pl.ds(0, 16)], r.at[pl.ds(0, 16)]), i + 4, right2)
        send(lambda: (s.at[pl.ds(16, 16)], r.at[pl.ds(16, 16)]), i + 5, left2)

    def reduce4(p):
        s, r, i, o = S2[p], R2[p], ring_sem[p], OWN[p]
        recv(r.at[pl.ds(0, 16)], i + 4)
        s[pl.ds(32, 16), :] = (o[sub(1, 0, 16), :] + r[pl.ds(0, 16), :].astype(F32)).astype(BF)
        s[pl.ds(48, 16), :] = o[sub(1, 16, 16), :].astype(BF)
        send(lambda: (s.at[pl.ds(32, 32)], r.at[pl.ds(32, 32)]), i + 6, right2)
        recv(r.at[pl.ds(16, 16)], i + 5)
        s[pl.ds(64, 16), :] = o[sub(3, 0, 16), :].astype(BF)
        s[pl.ds(80, 16), :] = (o[sub(3, 16, 16), :] + r[pl.ds(16, 16), :].astype(F32)).astype(BF)
        send(lambda: (s.at[pl.ds(64, 32)], r.at[pl.ds(64, 32)]), i + 7, left2)

    def x_send(ref, base):
        for j in range(3):
            send(lambda: (ref().at[x], ref().at[x]), base + j, others_x[j])

    def x_recv(ref, base):
        for j in range(3):
            recv(ref().at[m4(x + 3 - j)], base + j)

    def reduce5(p):
        r, i, o = R2[p], ring_sem[p], OWN[p]
        recv(r.at[pl.ds(32, 32)], i + 6)
        recv(r.at[pl.ds(64, 32)], i + 7)
        total = o[sub(0), :] + r[pl.ds(32, 32), :].astype(F32) + r[pl.ds(64, 32), :].astype(F32)
        so[p] = total[:, 0:CPAD]
        if p:
            k12 = total[:, CPAD:]
            high = k12.astype(BF)
            kg[x, 0:32, :] = high
            kg[x, 32:64, :] = (k12 - high.astype(F32)).astype(BF)
            x_send(lambda: kg, kg_sem)

    lab_rows = pl.ds(pl.multiple_of(m4(feat) * 32, 32), 32)
    col = lax.broadcasted_iota(jnp.int32, (32, CPAD), 1)
    lane = lax.broadcasted_iota(jnp.int32, (32, 128), 1)

    def is_target(p):
        label = lt[p, lab_rows, 0:1].astype(jnp.int32) - x * CLS
        return (col == label) & (col < CLS)

    def find_target(p):
        if p:
            x_recv(lambda: kg, kg_sem)
            moved = jnp.zeros((64, CPAD), F32)
            for j in range(4):
                moved += jnp.dot(kg[j], gb[0, j * GRAM:(j + 1) * GRAM, :], preferred_element_type=F32)
            so[p] = so[p] - RATE * (moved[0:32] + moved[32:64])
        part = jnp.sum(jnp.where(is_target(p), so[p], 0.0), axis=1, keepdims=True)
        tg[p, x] = jnp.broadcast_to(part, (32, 128))
        x_send(lambda: tg.at[p], tg_sem[p])

    def find_margin(p):
        x_recv(lambda: tg.at[p], tg_sem[p])
        target = (tg[p, 0] + tg[p, 1] + tg[p, 2] + tg[p, 3])[:, 0:1]
        keep = (col < CLS) & jnp.logical_not(is_target(p))
        margin = jnp.where(keep, jnp.maximum(0.0, 1.0 + so[p] - target), 0.0)
        slope = margin * F32(2.0 / (NCLS - 1))
        so[p] = slope
        out = jnp.sum(slope, axis=1, keepdims=True)
        loss = jnp.sum(margin * margin, axis=1, keepdims=True) * F32(1.0 / (NCLS - 1))
        ox[p, x] = jnp.where(lane < 64, out, loss)
        x_send(lambda: ox.at[p], ox_sem[p])

    def find_grad(p):
        x_recv(lambda: ox.at[p], ox_sem[p])
        both = ox[p, 0] + ox[p, 1] + ox[p, 2] + ox[p, 3]
        out, loss = both[:, 0:1], both[:, 64:65]
        high = loss.astype(BF).astype(F32)
        mid = (loss - high).astype(BF).astype(F32)
        low = loss - high - mid
        g = jnp.where(is_target(p), -out, so[p])
        g = jnp.where(col == CLS, high, g)
        g = jnp.where(col == CLS + 1, mid, g)
        g = jnp.where(col == CLS + 2, low, g)
        gb[p, own(), :] = g.astype(BF)
        gg[p].step0()

    before = {
        1: [lambda: reduce0(0)],
        2: [lambda: reduce1(0)],
        3: [lambda: reduce2(0)],
        4: [lambda: reduce3(0)],
        5: [lambda: reduce5(0), lambda: find_target(0), lambda: reduce0(1)],
        6: [lambda: find_grad(0), lambda: reduce1(1)],
        7: [lambda: gg[0].step2(), lambda: reduce2(1)],
    }
    after = {
        1: [lambda: gx[1].step4()],
        2: [lambda: gx[1].step5()],
        4: [lambda: reduce4(0)],
        5: [lambda: find_margin(0)],
        6: [lambda: gg[0].step1()],
        7: [lambda: gg[0].step3()],
    }

    def run(tasks, s):
        for at_step, fns in tasks.items():

            @pl.when(s == at_step)
            def _(fns=fns):
                for fn in fns:
                    fn()

    def panel_step(s, _):
        p, k = s // 4, lax.rem(s, 4)
        d = 2 - k + 3 * (k // 2) - 2 * (k // 3)
        theirs = rows_at(1 - c, m4(p2 + d))
        mine = rows_at(c, m4(p1 + d))

        def feat_body(j, _):
            half = (1 - c) * (1 - j) + c * j
            blk = m4(p2 + d) * (1 - j) + m4(p1 + d) * j
            features(p, rows_at(half, blk))
            return 0

        lax.fori_loop(0, 2, feat_body, 0)
        run(before, s)
        ps[s] = scores(p, theirs).astype(BF)
        rc(ps.at[s], pr.at[s], pair_sem + s, partner).start()

        @pl.when(s >= 4)
        def _():
            psk[k] = gram(theirs).astype(BF)
            rc(psk.at[k], prk.at[k], pair_sem + 8 + k, partner).start()
            owk[k] = gram(mine)

        ows[k] = scores(p, mine)
        run(after, s)
        return 0

    lax.fori_loop(0, 8, panel_step, 0)
    for k in range(8):
        drain.append(lambda k=k: rc(ps.at[k], pr.at[k], pair_sem + k, partner).wait_send())
    for k in range(4):
        drain.append(lambda k=k: rc(psk.at[k], prk.at[k], pair_sem + 8 + k, partner).wait_send())

    f1_out = pltpu.make_async_copy(fb.at[1], f1_hbm, lsem.at[9])
    f1_out.start()
    reduce3(1)
    gg[0].step4()
    reduce4(1)
    gg[0].step5()
    reduce5(1)

    def wp_out(t):
        rows = pl.ds(pl.multiple_of(t * 256, 256), 256)
        return pltpu.make_async_copy(wf.at[rows], wp_hbm.at[rows], lsem.at[10])

    tail = {
        0: [lambda: find_target(1)],
        1: [lambda: find_margin(1)],
        2: [lambda: find_grad(1)],
        3: [lambda: gg[1].step1()],
        4: [lambda: gg[1].step2()],
        5: [lambda: gg[1].step3()],
        6: [lambda: gg[1].step4()],
        7: [lambda: gg[1].step5()],
    }

    def update_step(t, _):
        rows = pl.ds(pl.multiple_of(t * 256, 256), 256)
        gradient = lax.dot_general(
            fb[0, :, rows], gb[0], (((0,), (0,)), ((), ())), preferred_element_type=F32
        )
        wf[rows, :] = wf[rows, :] - RATE * gradient[:, 0:CLS]
        run(tail, t)
        return 0

    lax.fori_loop(0, 8, update_step, 0)
    wp_copy = pltpu.make_async_copy(wf, wp_hbm, lsem.at[10])
    wp_copy.start()
    g_out = pltpu.make_async_copy(gb, g_hbm, lsem.at[11])
    g_out.start()
    for fn in drain:
        fn()
    f1_out.wait()
    wp_copy.wait()
    g_out.wait()


def last_kernel(w, f, g, l0, l1, out, loss):
    gradient = lax.dot_general(f[...], g[0], (((0,), (0,)), ((), ())), preferred_element_type=F32)
    out[...] = w[...] - RATE * gradient[:, 0:CLS]

    @pl.when(pl.program_id(0) == 0)
    def _():
        lane = lax.broadcasted_iota(jnp.int32, (FRAMES, 128), 1)
        first = CLS - 1152
        here = (lane >= first) & (lane < first + 3)
        for p, ref in ((0, l0), (1, l1)):
            total = jnp.sum(jnp.where(here, ref[0].astype(F32), 0.0), axis=0, keepdims=True)
            total = jnp.sum(total, axis=1, keepdims=True)
            loss[pl.ds(p, 1), :] = jnp.broadcast_to(total, (1, 128))


def per_device(inputs, projection, offsets, labels, weights):
    vm = pl.BlockSpec(memory_space=pltpu.VMEM)
    hbm = pl.BlockSpec(memory_space=pl.ANY)
    v = pltpu.VMEM
    wide = (CPAD, CPAD + GRAM)
    f1, g, wp = pl.pallas_call(
        step_kernel,
        out_shape=(
            jax.ShapeDtypeStruct((FRAMES, FEATS), BF),
            jax.ShapeDtypeStruct((2, FRAMES, CPAD), BF),
            jax.ShapeDtypeStruct((FEATS, CLS), F32),
        ),
        in_specs=[vm, hbm, vm, vm, hbm],
        out_specs=(hbm, hbm, hbm),
        scratch_shapes=[
            v((2, FRAMES, DPAD), BF), v((DPAD, FEATS), BF), v((FEATS, CLS), F32), v((FEATS, CPAD), BF),
            v((2, FRAMES, FEATS), BF), v((4, 128, CPAD), F32), v((4, 128, GRAM), F32),
            v((8, 128, CPAD), BF), v((8, 128, CPAD), BF), v((4, 128, GRAM), BF), v((4, 128, GRAM), BF),
            *[v((3, 128, w), BF) for w in wide], *[v((384, w), BF) for w in wide],
            *[v((96, w), BF) for w in wide], *[v((96, w), BF) for w in wide],
            *[v((128, w), F32) for w in wide],
            v((2, 32, CPAD), F32), v((32, GRAM), F32), v((4, 64, GRAM), BF),
            v((2, 4, 32, 128), F32), v((2, 4, 32, 128), F32), v((2, 128, 128), F32),
            v((2, FRAMES, CPAD), BF),
            pltpu.SemaphoreType.DMA((96,)), pltpu.SemaphoreType.DMA((96,)), pltpu.SemaphoreType.DMA((12,)),
        ],
        compiler_params=pltpu.CompilerParams(collective_id=0, has_side_effects=True, vmem_limit_bytes=65 * 1000 * 1000),
        name="panels",
    )(inputs, projection, offsets.reshape(1, FEATS), labels, weights)
    new, loss = pl.pallas_call(
        last_kernel,
        grid=(8,),
        out_shape=(jax.ShapeDtypeStruct((FEATS, CLS), F32), jax.ShapeDtypeStruct((2, 128), F32)),
        in_specs=[
            pl.BlockSpec((256, CLS), lambda i: (i, 0)),
            pl.BlockSpec((FRAMES, 256), lambda i: (0, i)),
            pl.BlockSpec((1, FRAMES, CPAD), lambda i: (1, 0, 0)),
            pl.BlockSpec((1, FRAMES, 128), lambda i: (0, 0, 9)),
            pl.BlockSpec((1, FRAMES, 128), lambda i: (1, 0, 9)),
        ],
        out_specs=(pl.BlockSpec((256, CLS), lambda i: (i, 0)), pl.BlockSpec((2, 128), lambda i: (0, 0))),
        compiler_params=pltpu.CompilerParams(vmem_limit_bytes=48 * 2**20),
        name="last_update",
    )(wp, f1, g, g, g)
    return new, loss[:, 0]


def solution(mesh):
    return jax.shard_map(
        per_device,
        mesh=mesh,
        in_specs=(P(None, "feat", None), P(None, "feat"), P("feat"), P(), P("feat", "cls")),
        out_specs=(P("feat", "cls"), P()),
        check_vma=False,
    )
```

time: 404 us -> 167 us (0.41); the launches traced: 399 us -> 167 us
  waiting for transfers between devices: 174 us -> 0 us
  Pallas kernels: 0 us -> 141 us
  matrix products: 101 us -> 0 us
  blocking collectives: 85.7 us -> 0 us
  local copies, waits for them, and re-layouts: 6.8 us -> 25.1 us
  other arithmetic: 17.2 us -> 0 us
  between operations: 14.2 us -> 0.65 us
    psum x2 -> x0, waiting for transfers between devices: 174 us -> none  [per_device(): lax.psum(jnp.dot(features, narrow, preferred_element_type=jnp.float32), '...]
    pallas_call x0 -> x2, Pallas kernels: none -> 141 us  [the longest x1 127 us: per_device(): pl.pallas_call(step_kernel, out_shape=(jax.ShapeDtypeStruct((FRAMES, FEAT...]
    dot_general x6 -> x0, matrix products: 101 us -> none  [the longest x2 61.7 us: per_device(): jnp.dot(lax.all_gather(inputs[panel_index], 'feat', axis=0, tiled=True),...]
    all_gather x2 -> x0, blocking collectives: 52.1 us -> none  [per_device(): lax.all_gather(inputs[panel_index], 'feat', axis=0, tiled=True)]
    psum x4 -> x0, blocking collectives: 33.6 us -> none  [the longest x2 16.8 us: per_device(): target = lax.psum(jnp.sum(jnp.where(is_target, scores, 0.0), axis=1), 'cls')]
    unnamed x12 -> x4, local copies, waits for them, and re-layouts: 6.03 us -> 24.5 us
    reduce_sum x6 -> x0, other arithmetic: 14.5 us -> none  [the longest x2 7.11 us: per_device(): jnp.sum(margin * margin, axis=1) / (NCLS - 1)]
  transfers between devices with their start and end apart: 2 -> 0, of which waited for: 2 -> 0; matrix products, arithmetic and copies ran while one was open for 8% -> 0% of each run, Pallas kernels for 0% -> 0%
where the time goes in v1:
time: 167 us
  Pallas kernels  141 us (84%)
  local copies, waits for them, and re-layouts  25.1 us (15%)
    pallas_call x1, Pallas kernels, per_device(): pl.pallas_call(step_kernel, out_shape=(jax.ShapeDtypeStruct((FRAMES, FEAT...  127 us
    unnamed x4, local copies, waits for them, and re-layouts  24.5 us
    pallas_call x1, Pallas kernels, per_device(): pl.pallas_call(last_kernel, grid=(8,), out_shape=(jax.ShapeDtypeStruct((F...  13.8 us

profile of v1, /device:TPU:1, one launch (start us, length us, event | category | flops | bytes accessed | tf_op | source)
XLA Modules:
  0.0 166.6 jit_solution(7661287815167604786)
XLA Ops:
  0.6 11.2 %copy.9.w_hbm = f32[2048,1250]{1,0:T(8,128)} copy(f32[2048,1250]{0,1:T(8,128)} %param.9) | data formatting | bytes 20480000 | tf_op args[4]
  11.8 127.0 %panels.1 = (bf16[1024,2048]{1,0:T(8,128)(2,1)}, bf16[2,1024,1280]{2,1,0:T(8,128)(2,1)}, f32[2048,1250]{1,0:T(8,128)}) custom-call(bf16[2,32,360]{2,1,0:T(8,128)(2,1)} %inp.1, bf16[360,2048]{1,0:T(8,128)(2,1)} %proj.1, s32[1,2048]{1,0:T(1,128)} %bitcast.1, s32[2,1024]{1,0:T(2,128)} %lab.1, f32[2048,1250]{1,0:T(8,128)} %copy.9.w_hbm), custom_call_target="tpu_custom_call" | custom-call | tf_op jit(solution)/shard_map/panels/pallas_call | solution.py:475
  138.8 0.0 copy-start
  138.8 2.2 %copy-done = bf16[1024,2048]{1,0:T(8,128)(2,1)S(1)} copy-done((bf16[1024,2048]{1,0:T(8,128)(2,1)S(1)}, bf16[1024,2048]{1,0:T(8,128)(2,1)}, u32[]{:S(2)}) %copy-start) | copy-done | bytes 4194328
  141.0 13.8 %last_update.1 = (f32[2048,1250]{1,0:T(8,128)}, f32[2,128]{1,0:T(2,128)S(1)}) custom-call(f32[2048,1250]{1,0:T(8,128)} %get-tuple-element.7.w, bf16[1024,2048]{1,0:T(8,128)(2,1)S(1)} %copy-done, bf16[2,1024,1280]{2,1,0:T(8,128)(2,1)} %get-tuple-element.9.g.l0.l1, bf16[2,1024,1280]{2,1,0:T(8,128)(2,1)} %get-tuple-element.9.g.l0.l1, ...), custom_call_target="tpu_custom_call" | custom-call | tf_op jit(solution)/shard_map/last_update/pallas_call | solution.py:499
  154.8 11.1 %copy.10 = f32[2048,1250]{0,1:T(8,128)} copy(f32[2048,1250]{1,0:T(8,128)} %get-tuple-element.14) | data formatting | bytes 20480000
  165.9 0.6 slice_reduce_fusion
Async XLA Ops:
  138.8 2.2 %copy-start = (bf16[1024,2048]{1,0:T(8,128)(2,1)S(1)}, bf16[1024,2048]{1,0:T(8,128)(2,1)}, u32[]{:S(2)}) copy-start(bf16[1024,2048]{1,0:T(8,128)(2,1)} %get-tuple-element.8.f) | copy-start | bytes 12582916

commit v2 on v1

v2 whole, which is shorter than its diff:
```python
import math

import jax
import jax.numpy as jnp
from jax import lax
from jax.experimental import pallas as pl
from jax.experimental.pallas import tpu as pltpu
from jax.sharding import PartitionSpec as P

DIN, DPAD = 360, 384
NFEAT = 65536
NCLS = 5000
FRAMES = 1024
FEATS = 2048
CLS = 1250
CPAD = 1280
GRAM = 256
TILES = 10
LAST = 1152
SEMS = 192
WIDE = (CPAD, CPAD + GRAM)
RATE = 10.0
MESH = pl.DeviceIdType.MESH
BF, F32 = jnp.bfloat16, jnp.float32
SINE = (6.2831851595779975, -41.34165492085313, 81.60099762206104, -76.54964291002278, 39.53570242669577)


def m4(v):
    return lax.rem(v, 4)


def step_kernel(
    inp, proj, off, lab, w_hbm,
    f1_hbm, g_hbm, wp_hbm,
    xb, pb, wf, tail_rows, wn, fb, ows, ps, pr,
    s1_0, s1_1, r1_0, r1_1, s2_0, s2_1, r2_0, r2_1, own_0, own_1,
    so, kg, tg, ox, lt, gb, ssem, rsem, lsem,
):
    feat, x = lax.axis_index("feat"), lax.axis_index("cls")
    c = lax.rem(feat, 2)
    y = m4(feat // 2)
    z = feat // 8
    p1 = y * (1 - c) + z * c
    p2 = z * (1 - c) + y * c

    def at(a, b):
        return ((b * (1 - c) + a * c) * 8 + (a * (1 - c) + b * c) * 2 + c, x)

    right1, left1 = at(m4(p1 + 1), p2), at(m4(p1 + 3), p2)
    across1 = at(m4(p1 + 2), p2)
    ring2 = [at(p1, m4(p2 + d)) for d in (1, 2, 3)]
    partner = (feat + 1 - 2 * c, x)
    others_x = [(feat, m4(x + j)) for j in (1, 2, 3)]

    drain = []

    def rc(src, dst, i, dev, j=None):
        return pltpu.make_async_remote_copy(
            src_ref=src,
            dst_ref=dst,
            send_sem=ssem.at[i],
            recv_sem=rsem.at[i if j is None else j],
            device_id=dev,
            device_id_type=MESH,
        )

    def send(ends, i, dev, j=None):
        rc(*ends(), i, dev, j).start()
        drain.append(lambda: rc(*ends(), i, dev, j).wait_send())

    def recv(region, i):
        rc(region, region, i, partner).wait_recv()

    counter = [0]

    def sems(n):
        counter[0] += n
        return counter[0] - n

    def rows_at(cc, b1, b2=0, extra=0, size=128):
        start = cc * 512 + b1 * 128 + b2 * 32 + extra
        return pl.ds(pl.multiple_of(start, min(size, 128)), size)

    w_in = pltpu.make_async_copy(w_hbm, wf, lsem.at[4])
    proj_in = pltpu.make_async_copy(proj, pb.at[pl.ds(0, DIN)], lsem.at[0])
    proj_in.start()
    w_in.start()
    tail_rows[...] = jnp.zeros((128, FEATS), F32)

    own = lambda: rows_at(c, p1, p2, 0, 32)
    for p in range(2):
        xb[p, own(), :] = jnp.zeros((32, DPAD), BF)
        xb[p, own(), 0:DIN] = inp[p]

    barrier = pltpu.get_barrier_semaphore()
    for dev in [right1, left1, across1, partner] + ring2 + others_x:
        pl.semaphore_signal(barrier, inc=1, device_id=dev, device_id_type=MESH)
    pl.semaphore_wait(barrier, 10)

    class Gather:
        def __init__(self, buf, direct):
            self.buf, self.direct = buf, direct
            self.base = sems(36)
            self.sent = 0

        def put(self, rows, i, dev):
            send(lambda: (self.buf().at[rows()], self.buf().at[rows()]), self.base + i, dev)

        def take(self, rows, i):
            recv(self.buf().at[rows()], self.base + i)

        def pass_on(self, rows):
            i = self.base + 23 + self.sent
            self.sent += 1
            send(lambda: (self.buf().at[rows()], self.buf().at[rows()]), i, partner, self.base + 23)

        def out1(self, j):
            rows = lambda: rows_at(c, p1, m4(p2 + j), 0, 32)
            self.put(rows, 3 + 3 * j, right1)
            self.put(rows, 5 + 3 * j, left1)
            if self.direct:
                self.put(rows, 4 + 3 * j, across1)
            self.pass_on(rows)

        def in1(self, j):
            b2 = m4(p2 + j)
            self.take(lambda: rows_at(c, m4(p1 + 3), b2, 0, 32), 3 + 3 * j)
            if not self.direct:
                self.put(lambda: rows_at(c, m4(p1 + 3), m4(p2 + j), 0, 16), 15 + 2 * j, right1)
            self.pass_on(lambda: rows_at(c, m4(p1 + 3), m4(p2 + j), 0, 32))
            self.take(lambda: rows_at(c, m4(p1 + 1), b2, 0, 32), 5 + 3 * j)
            if not self.direct:
                self.put(lambda: rows_at(c, m4(p1 + 1), m4(p2 + j), 16, 16), 16 + 2 * j, left1)
            self.pass_on(lambda: rows_at(c, m4(p1 + 1), m4(p2 + j), 0, 32))

        def step0(self):
            for d in (2, 1, 3):
                self.put(own, d - 1, ring2[d - 1])
            self.out1(0)

        def step1(self):
            for d in (1, 3, 2):
                self.take(lambda: rows_at(c, p1, m4(p2 + 4 - d), 0, 32), d - 1)
                self.out1(4 - d)

        def step2(self):
            self.in1(0)

        def step3(self):
            for j in (3, 1, 2):
                self.in1(j)

        def step4(self):
            for j in range(4):
                b2 = m4(p2 + j)
                if self.direct:
                    self.take(lambda: rows_at(c, m4(p1 + 2), b2, 0, 32), 4 + 3 * j)
                else:
                    self.take(lambda: rows_at(c, m4(p1 + 2), b2, 0, 16), 15 + 2 * j)
                    self.take(lambda: rows_at(c, m4(p1 + 2), b2, 16, 16), 16 + 2 * j)
            self.pass_on(lambda: rows_at(c, m4(p1 + 2)))

        def step5(self):
            self.take(lambda: rows_at(1 - c, 0, 0, 0, 512), 23)

    gx = [Gather(lambda p=p: xb.at[p], True) for p in range(2)]
    gg = [Gather(lambda p=p: gb.at[p], False) for p in range(2)]

    gx[0].step0()

    pb[DIN:DPAD, :] = jnp.zeros((DPAD - DIN, FEATS), BF)
    turns = off[...].astype(F32) * F32(1.0 / 65521.0)
    lab_col = pl.multiple_of((feat // 4) * 128, 128)
    for p in range(2):
        row = lab[pl.ds(p, 1), pl.ds(lab_col, 128)].astype(F32)
        lt[p] = jnp.broadcast_to(row, (128, 128)).T
    def narrow(t):
        if t < TILES - 1:
            rows = wf[pl.ds(t * 128, 128), :]
        else:
            tail_rows[0:CLS - LAST, :] = wf[LAST:CLS, :]
            rows = tail_rows[...]
        wn[:, t * 128:t * 128 + 128] = rows.astype(BF).T

    w_in.wait()
    for t in range(5):
        narrow(t)
    gx[0].step1()
    gx[1].step0()
    for t in range(5, 8):
        narrow(t)
    gx[0].step2()
    gx[0].step3()
    gx[0].step4()
    for t in range(8, TILES):
        narrow(t)
    gx[1].step1()
    proj_in.wait()
    gx[0].step5()

    scale = math.sqrt(2.0 / NFEAT)
    coef = [F32(v * scale) for v in SINE]

    def features(p, rows):
        acc = jnp.dot(xb[p, rows, :], pb[...], preferred_element_type=F32)
        u = acc * F32(1.0 / (2.0 * math.pi)) + turns
        q = jnp.abs(u - jnp.round(u)) - 0.25
        q2 = q * q
        r = coef[4]
        for v in coef[3::-1]:
            r = r * q2 + v
        fb[p, rows, :] = (r * q).astype(BF)

    def scores(p, rows):
        return jnp.dot(fb[p, rows, :], wn[:, 0:WIDE[p]], preferred_element_type=F32)

    S1, R1, S2, R2, OWN = (s1_0, s1_1), (r1_0, r1_1), (s2_0, s2_1), (r2_0, r2_1), (own_0, own_1)
    pair_sem = sems(8)
    ring_sem = [sems(8), sems(8)]
    tg_sem, ox_sem, kg_sem = [sems(3), sems(3)], [sems(3), sems(3)], sems(3)

    def pair_recv(p, k):
        recv(pr.at[4 * p + k, :, pl.ds(0, WIDE[p])], pair_sem + 4 * p + k)

    def combine(p, k, put, lo, hi):
        def body(i, _):
            rows = pl.ds(pl.multiple_of(i * 32, 32), 32)
            put(rows, slice(0, WIDE[p]), ows[k, rows, 0:WIDE[p]] + pr[4 * p + k, rows, 0:WIDE[p]].astype(F32))
            return 0

        lax.fori_loop(lo, hi, body, 0)

    def reduce0(p):
        pair_recv(p, 0)
        s, r, i = S1[p], R1[p], ring_sem[p]

        def put(rows, cols, v):
            s[0, rows, cols] = v.astype(BF)

        combine(p, 0, put, 0, 4)
        send(lambda: (s.at[0, pl.ds(0, 64)], r.at[pl.ds(0, 64)]), i, right1)
        send(lambda: (s.at[0, pl.ds(64, 64)], r.at[pl.ds(64, 64)]), i + 1, left1)

    def reduce1(p):
        pair_recv(p, 1)
        s, r, i = S1[p], R1[p], ring_sem[p]
        recv(r.at[pl.ds(0, 64)], i)

        def put_in(rows, cols, v):
            s[1, rows, cols] = (v + r[rows, cols].astype(F32)).astype(BF)

        def put(rows, cols, v):
            s[1, rows, cols] = v.astype(BF)

        combine(p, 1, put_in, 0, 2)
        combine(p, 1, put, 2, 4)
        send(lambda: (s.at[1], r.at[pl.ds(128, 128)]), i + 2, right1)

    def reduce2(p):
        pair_recv(p, 2)
        s, r, i = S1[p], R1[p], ring_sem[p]
        recv(r.at[pl.ds(64, 64)], i + 1)

        def put_in(rows, cols, v):
            s[2, rows, cols] = (v + r[rows, cols].astype(F32)).astype(BF)

        def put(rows, cols, v):
            s[2, rows, cols] = v.astype(BF)

        combine(p, 2, put, 0, 2)
        combine(p, 2, put_in, 2, 4)
        send(lambda: (s.at[2], r.at[pl.ds(256, 128)]), i + 3, left1)

    def sub(d, extra=0, size=32):
        return pl.ds(pl.multiple_of(m4(p2 + d) * 32 + extra, 16), size)

    def reduce3(p):
        pair_recv(p, 3)
        r, i, o = R1[p], ring_sem[p], OWN[p]
        recv(r.at[pl.ds(128, 128)], i + 2)
        recv(r.at[pl.ds(256, 128)], i + 3)

        def put(rows, cols, v):
            a = pl.ds(pl.multiple_of(rows.start + 128, 32), 32)
            b = pl.ds(pl.multiple_of(rows.start + 256, 32), 32)
            o[rows, cols] = v + r[a, cols].astype(F32) + r[b, cols].astype(F32)

        combine(p, 3, put, 0, 4)
        s, r = S2[p], R2[p]
        for d in (2, 1, 3):
            piece = pl.ds(32 * d - 32, 32)
            s[piece, :] = o[sub(d), :].astype(BF)
            send(lambda piece=piece: (s.at[piece], r.at[piece]), i + 3 + d, ring2[d - 1])

    def x_send(ref, base):
        for j in range(3):
            send(lambda: (ref().at[x], ref().at[x]), base + j, others_x[j])

    def x_recv(ref, base):
        for j in range(3):
            recv(ref().at[m4(x + 3 - j)], base + j)

    def reduce5(p):
        r, i, o = R2[p], ring_sem[p], OWN[p]
        total = o[sub(0), :]
        for d in (1, 3, 2):
            piece = pl.ds(32 * d - 32, 32)
            recv(r.at[piece], i + 3 + d)
            total += r[piece, :].astype(F32)
        so[p] = total[:, 0:CPAD]
        if p:
            k12 = total[:, CPAD:]
            high = k12.astype(BF)
            kg[x, 0:32, :] = high
            kg[x, 32:64, :] = (k12 - high.astype(F32)).astype(BF)
            x_send(lambda: kg, kg_sem)

    lab_rows = pl.ds(pl.multiple_of(m4(feat) * 32, 32), 32)
    col = lax.broadcasted_iota(jnp.int32, (32, CPAD), 1)
    lane = lax.broadcasted_iota(jnp.int32, (32, 128), 1)

    def is_target(p):
        label = lt[p, lab_rows, 0:1].astype(jnp.int32) - x * CLS
        return (col == label) & (col < CLS)

    def find_target(p):
        if p:
            x_recv(lambda: kg, kg_sem)
            moved = jnp.zeros((64, CPAD), F32)
            for j in range(4):
                moved += jnp.dot(kg[j], gb[0, j * GRAM:(j + 1) * GRAM, :], preferred_element_type=F32)
            so[p] = so[p] - RATE * (moved[0:32] + moved[32:64])
        part = jnp.sum(jnp.where(is_target(p), so[p], 0.0), axis=1, keepdims=True)
        tg[p, x] = jnp.broadcast_to(part, (32, 128))
        x_send(lambda: tg.at[p], tg_sem[p])

    def find_margin(p):
        x_recv(lambda: tg.at[p], tg_sem[p])
        target = (tg[p, 0] + tg[p, 1] + tg[p, 2] + tg[p, 3])[:, 0:1]
        keep = (col < CLS) & jnp.logical_not(is_target(p))
        margin = jnp.where(keep, jnp.maximum(0.0, 1.0 + so[p] - target), 0.0)
        slope = margin * F32(2.0 / (NCLS - 1))
        so[p] = slope
        out = jnp.sum(slope, axis=1, keepdims=True)
        loss = jnp.sum(margin * margin, axis=1, keepdims=True) * F32(1.0 / (NCLS - 1))
        ox[p, x] = jnp.where(lane < 64, out, loss)
        x_send(lambda: ox.at[p], ox_sem[p])

    def find_grad(p):
        x_recv(lambda: ox.at[p], ox_sem[p])
        both = ox[p, 0] + ox[p, 1] + ox[p, 2] + ox[p, 3]
        out, loss = both[:, 0:1], both[:, 64:65]
        high = loss.astype(BF).astype(F32)
        mid = (loss - high).astype(BF).astype(F32)
        low = loss - high - mid
        g = jnp.where(is_target(p), -out, so[p])
        g = jnp.where(col == CLS, high, g)
        g = jnp.where(col == CLS + 1, mid, g)
        g = jnp.where(col == CLS + 2, low, g)
        gb[p, own(), :] = g.astype(BF)
        gg[p].step0()

    before = {
        1: [lambda: reduce0(0)],
        2: [lambda: reduce1(0)],
        3: [lambda: reduce2(0)],
        4: [lambda: reduce3(0)],
        5: [lambda: reduce5(0), lambda: find_target(0), lambda: reduce0(1)],
        6: [lambda: find_grad(0), lambda: reduce1(1)],
        7: [lambda: gg[0].step1(), lambda: reduce2(1)],
    }
    between = {
        0: [lambda: gx[1].step2()],
        1: [lambda: gx[1].step3()],
        2: [lambda: gx[1].step4()],
        3: [lambda: gx[1].step5()],
        7: [lambda: gg[0].step2()],
    }
    after = {
        5: [lambda: find_margin(0)],
    }

    def run(tasks, s, panel=None):
        for at_step, fns in tasks.items():
            if panel is not None and at_step // 4 != panel:
                continue

            @pl.when(s == at_step)
            def _(fns=fns):
                for fn in fns:
                    fn()

    def panel_step(s, _):
        p, k = s // 4, lax.rem(s, 4)
        d = 2 - k + 3 * (k // 2) - 2 * (k // 3)
        theirs = rows_at(1 - c, m4(p2 + d))
        mine = rows_at(c, m4(p1 + d))

        def feat_body(j, _):
            half = (1 - c) * (1 - j) + c * j
            blk = m4(p2 + d) * (1 - j) + m4(p1 + d) * j
            features(p, rows_at(half, blk))
            return 0

        lax.fori_loop(0, 2, feat_body, 0)
        run(before, s)
        quarter = pl.ds(pl.multiple_of(x * GRAM, GRAM), GRAM)

        @pl.when(s == 4)
        def _():
            wn[:, CPAD:] = fb[0, quarter, :].T

        def both(p):
            cols = pl.ds(0, WIDE[p])
            ps[s, :, cols] = scores(p, theirs).astype(BF)
            rc(ps.at[s, :, cols], pr.at[s, :, cols], pair_sem + s, partner).start()
            run(between, s, p)
            ows[k, :, cols] = scores(p, mine)

        pl.when(s < 4)(lambda: both(0))
        pl.when(s >= 4)(lambda: both(1))
        run(after, s)
        return 0

    lax.fori_loop(0, 8, panel_step, 0)

    def pair_done(k):
        cols = pl.ds(0, WIDE[k // 4])
        rc(ps.at[k, :, cols], pr.at[k, :, cols], pair_sem + k, partner).wait_send()

    for k in range(8):
        drain.append(lambda k=k: pair_done(k))

    f1_out = pltpu.make_async_copy(fb.at[1], f1_hbm, lsem.at[1])
    f1_out.start()
    reduce3(1)
    gg[0].step3()
    reduce5(1)
    gg[0].step4()
    gg[0].step5()
    g0_out = pltpu.make_async_copy(gb.at[0], g_hbm.at[0], lsem.at[4])
    g0_out.start()

    tail = {
        1: [lambda: find_target(1)],
        4: [lambda: find_margin(1)],
        7: [lambda: find_grad(1)],
    }

    def first_gradient(tile):
        return lax.dot_general(gb[0, :, tile], fb[0], (((0,), (0,)), ((), ())), preferred_element_type=F32)

    def update_step(t, _):
        tile = pl.ds(pl.multiple_of(t * 128, 128), 128)
        wf[tile, :] = wf[tile, :] - RATE * first_gradient(tile)
        pltpu.make_async_copy(wf.at[tile], wp_hbm.at[tile], lsem.at[2]).start()
        run(tail, t)
        return 0

    lax.fori_loop(0, TILES - 1, update_step, 0)
    tail_rows[...] = tail_rows[...] - RATE * first_gradient(pl.ds(LAST, 128))
    wp_last = pltpu.make_async_copy(tail_rows, wp_hbm.at[pl.ds(LAST, 128)], lsem.at[5])
    wp_last.start()
    gg[1].step1()
    gg[1].step2()
    gg[1].step3()
    gg[1].step4()
    gg[1].step5()
    g1_out = pltpu.make_async_copy(gb.at[1], g_hbm.at[1], lsem.at[3])
    g1_out.start()
    for fn in drain:
        fn()
    f1_out.wait()
    most = pl.ds(0, LAST)
    pltpu.make_async_copy(wf.at[most], wp_hbm.at[most], lsem.at[2]).wait()
    wp_last.wait()
    g0_out.wait()
    g1_out.wait()


def last_kernel(w, f, g, l0, l1, out, loss):
    gradient = lax.dot_general(g[0], f[...], (((0,), (0,)), ((), ())), preferred_element_type=F32)
    out[...] = w[...] - RATE * gradient

    @pl.when(pl.program_id(0) == 0)
    def _():
        lane = lax.broadcasted_iota(jnp.int32, (FRAMES, 128), 1)
        first = CLS - 1152
        here = (lane >= first) & (lane < first + 3)
        for p, ref in ((0, l0), (1, l1)):
            loss[p] = jnp.sum(jnp.where(here, ref[0].astype(F32), 0.0))


def per_device(inputs, projection, offsets, labels, weights):
    vm = pl.BlockSpec(memory_space=pltpu.VMEM)
    hbm = pl.BlockSpec(memory_space=pl.ANY)
    v = pltpu.VMEM
    wide = WIDE
    f1, g, wp = pl.pallas_call(
        step_kernel,
        out_shape=(
            jax.ShapeDtypeStruct((FRAMES, FEATS), BF),
            jax.ShapeDtypeStruct((2, FRAMES, CPAD), BF),
            jax.ShapeDtypeStruct((CPAD, FEATS), F32),
        ),
        in_specs=[vm, hbm, vm, vm, hbm],
        out_specs=(hbm, hbm, hbm),
        scratch_shapes=[
            v((2, FRAMES, DPAD), BF), v((DPAD, FEATS), BF), v((CLS, FEATS), F32), v((128, FEATS), F32), v((FEATS, WIDE[1]), BF),
            v((2, FRAMES, FEATS), BF), v((4, 128, WIDE[1]), F32),
            v((8, 128, WIDE[1]), BF), v((8, 128, WIDE[1]), BF),
            *[v((3, 128, w), BF) for w in wide], *[v((384, w), BF) for w in wide],
            *[v((96, w), BF) for w in wide], *[v((96, w), BF) for w in wide],
            *[v((128, w), F32) for w in wide],
            v((2, 32, CPAD), F32), v((4, 64, GRAM), BF),
            v((2, 4, 32, 128), F32), v((2, 4, 32, 128), F32), v((2, 128, 128), F32),
            v((2, FRAMES, CPAD), BF),
            pltpu.SemaphoreType.DMA((SEMS,)), pltpu.SemaphoreType.DMA((SEMS,)), pltpu.SemaphoreType.DMA((6,)),
        ],
        compiler_params=pltpu.CompilerParams(collective_id=0, has_side_effects=True, vmem_limit_bytes=65 * 1000 * 1000),
        name="panels",
    )(inputs, projection, offsets.reshape(1, FEATS), labels, weights.T)
    new, loss = pl.pallas_call(
        last_kernel,
        grid=(5,),
        out_shape=(jax.ShapeDtypeStruct((CLS, FEATS), F32), jax.ShapeDtypeStruct((2,), F32)),
        in_specs=[
            pl.BlockSpec((256, FEATS), lambda i: (i, 0)),
            pl.BlockSpec((FRAMES, FEATS), lambda i: (0, 0)),
            pl.BlockSpec((1, FRAMES, 256), lambda i: (1, 0, i)),
            pl.BlockSpec((1, FRAMES, 128), lambda i: (0, 0, 9)),
            pl.BlockSpec((1, FRAMES, 128), lambda i: (1, 0, 9)),
        ],
        out_specs=(pl.BlockSpec((256, FEATS), lambda i: (i, 0)), pl.BlockSpec(memory_space=pltpu.SMEM)),
        compiler_params=pltpu.CompilerParams(vmem_limit_bytes=62 * 2**20),
        name="last_update",
    )(wp, f1, g, g, g)
    return new.T, loss


def solution(mesh):
    return jax.shard_map(
        per_device,
        mesh=mesh,
        in_specs=(P(None, "feat", None), P(None, "feat"), P("feat"), P(), P("feat", "cls")),
        out_specs=(P("feat", "cls"), P()),
        check_vma=False,
    )
```

time: 167 us -> 123 us (0.74)
  local copies, waits for them, and re-layouts: 25.1 us -> 0 us
  Pallas kernels: 141 us -> 122 us
    unnamed x4 -> x0, local copies, waits for them, and re-layouts: 24.5 us -> none
    pallas_call x1, Pallas kernels: 127 us -> 108 us  [per_device(): pl.pallas_call(step_kernel, out_shape=(jax.ShapeDtypeStruct((FRAMES, FEAT...]
where the time goes in v2:
time: 123 us
  Pallas kernels  122 us (99%)
    pallas_call x1, Pallas kernels, per_device(): pl.pallas_call(step_kernel, out_shape=(jax.ShapeDtypeStruct((FRAMES, FEAT...  108 us
    pallas_call x1, Pallas kernels, per_device(): pl.pallas_call(last_kernel, grid=(5,), out_shape=(jax.ShapeDtypeStruct((C...  14.6 us

profile of v2, /device:TPU:1, one launch (start us, length us, event | category | flops | bytes accessed | tf_op | source)
XLA Modules:
  0.0 122.8 jit_solution(14863948849604645902)
XLA Ops:
  0.6 107.5 %panels.1 = (bf16[1024,2048]{1,0:T(8,128)(2,1)}, bf16[2,1024,1280]{2,1,0:T(8,128)(2,1)}, f32[1280,2048]{1,0:T(8,128)}) custom-call(bf16[2,32,360]{2,1,0:T(8,128)(2,1)} %inp.1, bf16[360,2048]{1,0:T(8,128)(2,1)} %proj.1, s32[1,2048]{1,0:T(1,128)} %bitcast.4, s32[2,1024]{1,0:T(2,128)} %lab.1, f32[1250,2048]{1,0:T(8,128)} %bitcast.3), custom_call_target="tpu_custom_call" | custom-call | tf_op jit(solution)/shard_map/panels/pallas_call | solution.py:499
  108.1 14.6 %last_update.1 = (f32[1250,2048]{1,0:T(8,128)}, f32[2]{0:T(128)}) custom-call(f32[1280,2048]{1,0:T(8,128)} %get-tuple-element.7.w, bf16[1024,2048]{1,0:T(8,128)(2,1)} %get-tuple-element.8.f, bf16[2,1024,1280]{2,1,0:T(8,128)(2,1)} %get-tuple-element.9.g.l0.l1, bf16[2,1024,1280]{2,1,0:T(8,128)(2,1)} %get-tuple-element.9.g.l0.l1, ...), custom_call_target="tpu_custom_call" | custom-call | tf_op jit(solution)/shard_map/last_update/pallas_call | solution.py:523

commit v3 on v2

v3 whole, which is shorter than its diff:
```python
import math

import jax
import jax.numpy as jnp
from jax import lax
from jax.experimental import pallas as pl
from jax.experimental.pallas import tpu as pltpu
from jax.sharding import PartitionSpec as P

DIN, DPAD = 360, 384
NFEAT = 65536
NCLS = 5000
FRAMES = 1024
FEATS = 2048
CLS = 1250
CPAD = 1280
GRAM = 256
TILES = 10
LAST = 1152
HALF = 640
SENDS, RECVS = 16, 96
WIDE = (CPAD, CPAD + GRAM)
RATE = 10.0
MESH = pl.DeviceIdType.MESH
BF, F32 = jnp.bfloat16, jnp.float32
SINE = (6.2831851595779975, -41.34165492085313, 81.60099762206104, -76.54964291002278, 39.53570242669577)


def m4(v):
    return lax.rem(v, 4)


def step_kernel(
    inp, proj, off, lab, w_hbm,
    f1_hbm, g1_hbm, l0_hbm, wp_hbm,
    xb, pb, wf, tail_rows, wn, fb, ows, ps, pr,
    s1_0, s1_1, r1_0, r1_1, s2_0, s2_1, r2_0, r2_1, own_0, own_1,
    so, kg, tg, ox, lt, lc, gb, ssem, rsem, lsem,
):
    feat, x = lax.axis_index("feat"), lax.axis_index("cls")
    c = lax.rem(feat, 2)
    y = m4(feat // 2)
    z = feat // 8
    p1 = y * (1 - c) + z * c
    p2 = z * (1 - c) + y * c

    def at(a, b):
        return ((b * (1 - c) + a * c) * 8 + (a * (1 - c) + b * c) * 2 + c, x)

    right1, left1 = at(m4(p1 + 1), p2), at(m4(p1 + 3), p2)
    across1 = at(m4(p1 + 2), p2)
    ring2 = [at(p1, m4(p2 + d)) for d in (1, 2, 3)]
    partner = (feat + 1 - 2 * c, x)
    others_x = [(feat, m4(x + j)) for j in (1, 2, 3)]

    drain = []

    def rc(src, dst, i, dev, j):
        return pltpu.make_async_remote_copy(
            src_ref=src,
            dst_ref=dst,
            send_sem=ssem.at[i],
            recv_sem=rsem.at[j],
            device_id=dev,
            device_id_type=MESH,
        )

    def sent(region, i):
        drain.append(lambda: rc(region(), region(), i, partner, 0).wait_send())

    def recv(region, i):
        rc(region, region, 0, partner, i).wait_recv()

    counter = [0]

    def sems(n):
        counter[0] += n
        return counter[0] - n

    group = [0]

    def send_sem():
        group[0] += 1
        return group[0] - 1

    def rows_at(cc, b1, b2=0, extra=0, size=128):
        start = cc * 512 + b1 * 128 + b2 * 32 + extra
        return pl.ds(pl.multiple_of(start, min(size, 128)), size)

    w_in = pltpu.make_async_copy(w_hbm, wf, lsem.at[4])
    proj_in = pltpu.make_async_copy(proj, pb.at[pl.ds(0, DIN)], lsem.at[0])
    proj_in.start()
    w_in.start()
    tail_rows[...] = jnp.zeros((128, FEATS), F32)

    own = lambda: rows_at(c, p1, p2, 0, 32)
    for p in range(2):
        xb[p, own(), :] = jnp.zeros((32, DPAD), BF)
        xb[p, own(), 0:DIN] = inp[p]

    barrier = pltpu.get_barrier_semaphore()
    for dev in [right1, left1, across1, partner] + ring2 + others_x:
        pl.semaphore_signal(barrier, inc=1, device_id=dev, device_id_type=MESH)
    pl.semaphore_wait(barrier, 10)

    class Gather:
        def __init__(self, buf, p, cols, direct):
            self.at = lambda rows: buf.at[p, rows, cols]
            self.direct = direct
            self.base, self.out = sems(13), send_sem()
            sent(lambda: self.at(pl.ds(0, 992)), self.out)

        def put(self, rows, i, dev):
            rc(self.at(rows()), self.at(rows()), self.out, dev, self.base + i).start()

        def take(self, rows, i):
            recv(self.at(rows()), self.base + i)

        def pass_on(self, rows):
            self.put(rows, 12, partner)

        def out1(self, j):
            rows = lambda: rows_at(c, p1, m4(p2 + j), 0, 32)
            self.put(rows, 3 + 2 * j, right1)
            self.put(rows, 4 + 2 * j, left1)
            if self.direct:
                self.put(rows, 11, across1)
            self.pass_on(rows)

        def in1(self, j):
            b2 = m4(p2 + j)
            self.take(lambda: rows_at(c, m4(p1 + 3), b2, 0, 32), 3 + 2 * j)
            if not self.direct:
                self.put(lambda: rows_at(c, m4(p1 + 3), b2, 0, 16), 11, right1)
            self.pass_on(lambda: rows_at(c, m4(p1 + 3), b2, 0, 32))
            self.take(lambda: rows_at(c, m4(p1 + 1), b2, 0, 32), 4 + 2 * j)
            if not self.direct:
                self.put(lambda: rows_at(c, m4(p1 + 1), b2, 16, 16), 11, left1)
            self.pass_on(lambda: rows_at(c, m4(p1 + 1), b2, 0, 32))

        def step0(self):
            for d in (2, 1, 3):
                self.put(own, d - 1, ring2[d - 1])
            self.out1(0)

        def step1(self):
            for d in (1, 3, 2):
                self.take(lambda: rows_at(c, p1, m4(p2 + 4 - d), 0, 32), d - 1)
                self.out1(4 - d)

        def step2(self):
            self.in1(0)

        def step3(self):
            for j in (3, 1, 2):
                self.in1(j)

        def step4(self):
            self.take(lambda: rows_at(c, m4(p1 + 2)), 11)
            self.pass_on(lambda: rows_at(c, m4(p1 + 2)))

        def step5(self):
            self.take(lambda: rows_at(1 - c, 0, 0, 0, 512), 12)

    gx = [Gather(xb, p, pl.ds(0, DPAD), True) for p in range(2)]
    gg = [Gather(gb, 0, pl.ds(0, CPAD), False)]
    ga = Gather(gb, 1, pl.ds(0, HALF), False)
    gz = Gather(gb, 1, pl.ds(HALF, CPAD - HALF), False)

    gx[0].step0()

    pb[DIN:DPAD, :] = jnp.zeros((DPAD - DIN, FEATS), BF)
    turns = off[...].astype(F32) * F32(1.0 / 65521.0)
    for q in range(FRAMES // 128):
        row = lab[0:1, q * 128:q * 128 + 128].astype(F32)
        turned = jnp.broadcast_to(row, (128, 128)).T
        for i in range(4):
            owner = 4 * q + i
            cc, yy, zz = owner % 2, owner // 2 % 4, owner // 8
            b1, b2 = (zz, yy) if cc else (yy, zz)
            start = cc * 512 + b1 * 128 + b2 * 32
            lc[start:start + 32, :] = turned[32 * i:32 * i + 32, :]
    lab_col = pl.multiple_of((feat // 4) * 128, 128)
    lt[...] = jnp.broadcast_to(lab[1:2, pl.ds(lab_col, 128)].astype(F32), (128, 128)).T

    def narrow(t):
        if t < TILES - 1:
            rows = wf[pl.ds(t * 128, 128), :]
        else:
            tail_rows[0:CLS - LAST, :] = wf[LAST:CLS, :]
            rows = tail_rows[...]
        wn[:, t * 128:t * 128 + 128] = rows.astype(BF).T

    w_in.wait()
    for t in range(5):
        narrow(t)
    gx[0].step1()
    gx[1].step0()
    for t in range(5, 8):
        narrow(t)
    gx[0].step2()
    gx[0].step3()
    gx[0].step4()
    for t in range(8, TILES):
        narrow(t)
    gx[1].step1()
    proj_in.wait()
    gx[0].step5()

    col = lax.broadcasted_iota(jnp.int32, (32, CPAD), 1)
    lane = lax.broadcasted_iota(jnp.int32, (32, 128), 1)
    scale = math.sqrt(2.0 / NFEAT)
    coef = [F32(v * scale) for v in SINE]

    def features(p, rows):
        acc = jnp.dot(xb[p, rows, :], pb[...], preferred_element_type=F32)
        u = acc * F32(1.0 / (2.0 * math.pi)) + turns
        q = jnp.abs(u - jnp.round(u)) - 0.25
        q2 = q * q
        r = coef[4]
        for v in coef[3::-1]:
            r = r * q2 + v
        fb[p, rows, :] = (r * q).astype(BF)

    def scores(p, rows):
        return jnp.dot(fb[p, rows, :], wn[:, 0:WIDE[p]], preferred_element_type=F32)

    S1, R1, S2, R2, OWN = (s1_0, s1_1), (r1_0, r1_1), (s2_0, s2_1), (r2_0, r2_1), (own_0, own_1)
    pair_sem = sems(8)
    ring_sem = [sems(7), sems(7)]
    tg_sem, ox_sem, kg_sem = [sems(1), sems(1)], [sems(1), sems(1)], sems(1)
    pair_out, ring_out, piece_out = ([send_sem(), send_sem()] for _ in range(3))
    tg_out, ox_out, kg_out = [send_sem(), send_sem()], [send_sem(), send_sem()], send_sem()
    three = pl.ds(0, 3)
    for p in range(2):
        sent(lambda p=p: ps.at[pl.ds(4 * p, 4), :, pl.ds(0, WIDE[p])], pair_out[p])
        sent(lambda p=p: R1[p], ring_out[p])
        sent(lambda p=p: R2[p], piece_out[p])
        sent(lambda p=p: tg.at[p, three], tg_out[p])
        sent(lambda p=p: ox.at[p, three], ox_out[p])
    sent(lambda: kg.at[three], kg_out)

    def pair_recv(p, k):
        recv(pr.at[4 * p + k, :, pl.ds(0, WIDE[p])], pair_sem + 4 * p + k)

    def apart(tile):
        at_lane = lax.broadcasted_iota(jnp.int32, tile.shape, 1)
        here = (at_lane == CLS - LAST) | (at_lane == CLS - LAST + 1)
        return jnp.sum(jnp.where(here, tile, 0.0), axis=1, keepdims=True)

    def rounded(p, v):
        if p:
            return v.astype(BF)
        tile = v[:, LAST:CPAD]
        at_lane = lax.broadcasted_iota(jnp.int32, tile.shape, 1)
        part = apart(tile)
        high = part.astype(BF).astype(F32)
        tile = jnp.where(at_lane == CLS - LAST, high, jnp.where(at_lane == CLS - LAST + 1, part - high, tile))
        return jnp.concatenate([v[:, 0:LAST], tile], axis=1).astype(BF)

    def mark_target(ref, i, rows):
        label = lc[rows, 0:1].astype(jnp.int32) - x * CLS
        label = jnp.where(label < CLS, label, -1)
        lane_at = lax.broadcasted_iota(jnp.int32, (128, 128), 1)
        found = jnp.zeros((128, 128), F32)
        for j in range(CPAD // 128):
            found += jnp.where(lane_at == label - j * 128, ref[i, :, j * 128:j * 128 + 128], 0.0)
        part = jnp.sum(found, axis=1, keepdims=True)
        ref[i, :, LAST:CPAD] = jnp.where(lane_at == CLS - LAST, part, ref[i, :, LAST:CPAD])

    def combine(p, k, put, lo, hi):
        def body(i, _):
            rows = pl.ds(pl.multiple_of(i * 32, 32), 32)
            put(rows, slice(0, WIDE[p]), ows[k, rows, 0:WIDE[p]] + pr[4 * p + k, rows, 0:WIDE[p]].astype(F32))
            return 0

        lax.fori_loop(lo, hi, body, 0)

    def reduce0(p):
        pair_recv(p, 0)
        s, r, i = S1[p], R1[p], ring_sem[p]

        def put(rows, cols, v):
            s[0, rows, cols] = rounded(p, v)

        combine(p, 0, put, 0, 4)
        rc(s.at[0, pl.ds(0, 64)], r.at[pl.ds(0, 64)], ring_out[p], right1, i).start()
        rc(s.at[0, pl.ds(64, 64)], r.at[pl.ds(64, 64)], ring_out[p], left1, i + 1).start()

    def reduce1(p):
        pair_recv(p, 1)
        s, r, i = S1[p], R1[p], ring_sem[p]
        recv(r.at[pl.ds(0, 64)], i)

        def put_in(rows, cols, v):
            s[1, rows, cols] = rounded(p, v + r[rows, cols].astype(F32))

        def put(rows, cols, v):
            s[1, rows, cols] = rounded(p, v)

        combine(p, 1, put_in, 0, 2)
        combine(p, 1, put, 2, 4)
        rc(s.at[1], r.at[pl.ds(128, 128)], ring_out[p], right1, i + 2).start()

    def reduce2(p):
        pair_recv(p, 2)
        s, r, i = S1[p], R1[p], ring_sem[p]
        recv(r.at[pl.ds(64, 64)], i + 1)

        def put_in(rows, cols, v):
            s[2, rows, cols] = rounded(p, v + r[rows, cols].astype(F32))

        def put(rows, cols, v):
            s[2, rows, cols] = rounded(p, v)

        combine(p, 2, put, 0, 2)
        combine(p, 2, put_in, 2, 4)
        rc(s.at[2], r.at[pl.ds(256, 128)], ring_out[p], left1, i + 3).start()

    def sub(d, extra=0, size=32):
        return pl.ds(pl.multiple_of(m4(p2 + d) * 32 + extra, 16), size)

    def reduce3(p):
        pair_recv(p, 3)
        r, i, o = R1[p], ring_sem[p], OWN[p]
        recv(r.at[pl.ds(128, 128)], i + 2)
        recv(r.at[pl.ds(256, 128)], i + 3)

        def put(rows, cols, v):
            a = pl.ds(pl.multiple_of(rows.start + 128, 32), 32)
            b = pl.ds(pl.multiple_of(rows.start + 256, 32), 32)
            o[rows, cols] = v + r[a, cols].astype(F32) + r[b, cols].astype(F32)

        combine(p, 3, put, 0, 4)
        s, r = S2[p], R2[p]
        for d in (2, 1, 3):
            piece = pl.ds(32 * d - 32, 32)
            s[piece, :] = rounded(p, o[sub(d), :])
            rc(s.at[piece], r.at[piece], piece_out[p], ring2[d - 1], i + 3 + d).start()

    def x_send(ref, out, i):
        for j in range(3):
            rc(ref.at[x], ref.at[x], out, others_x[j], i).start()

    def x_recv(ref, i):
        recv(ref.at[three], i)

    def reduce5(p):
        r, i, o = R2[p], ring_sem[p], OWN[p]
        total = o[sub(0), :]
        for d in (1, 3, 2):
            piece = pl.ds(32 * d - 32, 32)
            recv(r.at[piece], i + 3 + d)
            total += r[piece, :].astype(F32)
        so[p] = total[:, 0:CPAD]
        if p:
            k12 = total[:, CPAD:]
            high = k12.astype(BF)
            kg[x, 0:32, :] = high
            kg[x, 32:64, :] = (k12 - high.astype(F32)).astype(BF)
            x_send(kg, kg_out, kg_sem)

    lab_rows = pl.ds(pl.multiple_of(m4(feat) * 32, 32), 32)

    def is_target(p):
        label = (lt[lab_rows, 0:1] if p else lc[own(), 0:1]).astype(jnp.int32) - x * CLS
        return (col == label) & (col < CLS)

    def find_target(p):
        if p:
            x_recv(kg, kg_sem)
            moved = jnp.zeros((64, CPAD), F32)
            for j in range(4):
                moved += jnp.dot(kg[j], gb[0, j * GRAM:(j + 1) * GRAM, :], preferred_element_type=F32)
            so[p] = so[p] - RATE * (moved[0:32] + moved[32:64])
        if p:
            part = jnp.sum(jnp.where(is_target(p), so[p], 0.0), axis=1, keepdims=True)
        else:
            part = apart(so[0, :, LAST:])
        tg[p, x] = jnp.broadcast_to(part, (32, 128))
        x_send(tg.at[p], tg_out[p], tg_sem[p])

    def find_margin(p):
        x_recv(tg.at[p], tg_sem[p])
        target = (tg[p, 0] + tg[p, 1] + tg[p, 2] + tg[p, 3])[:, 0:1]
        keep = (col < CLS) & jnp.logical_not(is_target(p))
        margin = jnp.where(keep, jnp.maximum(0.0, 1.0 + so[p] - target), 0.0)
        slope = margin * F32(2.0 / (NCLS - 1))
        so[p] = slope
        out = jnp.sum(slope, axis=1, keepdims=True)
        loss = jnp.sum(margin * margin, axis=1, keepdims=True) * F32(1.0 / (NCLS - 1))
        ox[p, x] = jnp.where(lane < 64, out, loss)
        x_send(ox.at[p], ox_out[p], ox_sem[p])

    def find_grad(p):
        x_recv(ox.at[p], ox_sem[p])
        both = ox[p, 0] + ox[p, 1] + ox[p, 2] + ox[p, 3]
        out, loss = both[:, 0:1], both[:, 64:65]
        high = loss.astype(BF).astype(F32)
        mid = (loss - high).astype(BF).astype(F32)
        low = loss - high - mid
        g = jnp.where(is_target(p), -out, so[p])
        g = jnp.where(col == CLS, high, g)
        g = jnp.where(col == CLS + 1, mid, g)
        g = jnp.where(col == CLS + 2, low, g)
        gb[p, own(), :] = g.astype(BF)
        if p:
            ga.step0()
            gz.step0()
        else:
            gg[0].step0()

    before = {
        1: [lambda: reduce0(0)],
        2: [lambda: reduce1(0)],
        3: [lambda: reduce2(0)],
        4: [lambda: reduce3(0)],
        5: [lambda: reduce5(0), lambda: find_target(0), lambda: reduce0(1)],
        6: [lambda: find_grad(0), lambda: reduce1(1)],
        7: [lambda: reduce2(1), lambda: gg[0].step1()],
    }
    between = {
        0: [lambda: gx[1].step2()],
        1: [lambda: gx[1].step3()],
        2: [lambda: gx[1].step4()],
        3: [lambda: gx[1].step5()],
        7: [lambda: gg[0].step2()],
    }
    after = {
        5: [lambda: find_margin(0)],
    }

    def run(tasks, s, panel=None):
        for at_step, fns in tasks.items():
            if panel is not None and at_step // 4 != panel:
                continue

            @pl.when(s == at_step)
            def _(fns=fns):
                for fn in fns:
                    fn()

    def panel_step(s, _):
        p, k = s // 4, lax.rem(s, 4)
        d = 2 - k + 3 * (k // 2) - 2 * (k // 3)
        theirs = rows_at(1 - c, m4(p2 + d))
        mine = rows_at(c, m4(p1 + d))

        features(p, theirs)
        features(p, mine)
        run(before, s)
        quarter = pl.ds(pl.multiple_of(x * GRAM, GRAM), GRAM)

        @pl.when(s == 4)
        def _():
            wn[:, CPAD:] = fb[0, quarter, :].T

        def both(p):
            cols = pl.ds(0, WIDE[p])
            ps[s, :, cols] = scores(p, theirs)
            if p == 0:
                mark_target(ps, s, theirs)
            rc(ps.at[s, :, cols], pr.at[s, :, cols], pair_out[p], partner, pair_sem + s).start()
            run(between, s, p)
            ows[k, :, cols] = scores(p, mine)
            if p == 0:
                mark_target(ows, k, mine)

        pl.when(s < 4)(lambda: both(0))
        pl.when(s >= 4)(lambda: both(1))
        run(after, s)
        return 0

    lax.fori_loop(0, 8, panel_step, 0)

    f1_out = pltpu.make_async_copy(fb.at[1], f1_hbm, lsem.at[1])
    f1_out.start()
    reduce3(1)
    gg[0].step3()
    reduce5(1)
    gg[0].step4()
    gg[0].step5()
    g0_out = pltpu.make_async_copy(gb.at[0, :, pl.ds(LAST, 128)], l0_hbm, lsem.at[4])
    g0_out.start()

    tail = {
        1: [lambda: find_target(1)],
        4: [lambda: find_margin(1)],
        7: [lambda: find_grad(1)],
    }

    def gradient(p, tile):
        return lax.dot_general(gb[p, :, tile], fb[p], (((0,), (0,)), ((), ())), preferred_element_type=F32)

    def update_step(t, _):
        tile = pl.ds(pl.multiple_of(t * 128, 128), 128)
        wf[tile, :] = wf[tile, :] - RATE * gradient(0, tile)

        @pl.when(t >= HALF // 128)
        def _():
            pltpu.make_async_copy(wf.at[tile], wp_hbm.at[tile], lsem.at[2]).start()

        run(tail, t)
        return 0

    lax.fori_loop(0, TILES - 1, update_step, 0)
    tail_rows[...] = tail_rows[...] - RATE * gradient(0, pl.ds(LAST, 128))
    wp_last = pltpu.make_async_copy(tail_rows, wp_hbm.at[pl.ds(LAST, 128)], lsem.at[5])
    wp_last.start()
    ga.step1()
    gz.step1()
    ga.step2()
    ga.step3()
    gz.step2()
    gz.step3()
    ga.step4()
    ga.step5()
    second = {0: [lambda: gz.step4()]}

    def second_step(t, _):
        tile = pl.ds(pl.multiple_of(t * 128, 128), 128)
        run(second, t)
        wf[tile, :] = wf[tile, :] - RATE * gradient(1, tile)
        pltpu.make_async_copy(wf.at[tile], wp_hbm.at[tile], lsem.at[2]).start()
        return 0

    lax.fori_loop(0, HALF // 128, second_step, 0)
    gz.step5()
    g1_out = pltpu.make_async_copy(gb.at[1, :, pl.ds(HALF, CPAD - HALF)], g1_hbm, lsem.at[3])
    g1_out.start()
    for fn in drain:
        fn()
    f1_out.wait()
    most = pl.ds(0, LAST)
    pltpu.make_async_copy(wf.at[most], wp_hbm.at[most], lsem.at[2]).wait()
    wp_last.wait()
    g0_out.wait()
    g1_out.wait()


def block_of(i):
    return i // 2 + 5 * (1 - lax.rem(i, 2))


def last_kernel(w_hbm, f_hbm, g_hbm, l0, out, loss, wf, f, g, sem):
    i = pl.program_id(0)
    f_in = pltpu.make_async_copy(f_hbm, f, sem.at[0])
    g_in = pltpu.make_async_copy(g_hbm, g, sem.at[1])

    def load(t):
        rows = pl.ds(pl.multiple_of(t * 128, 128), 128)
        return pltpu.make_async_copy(w_hbm.at[rows], wf.at[rows], sem.at[2 + t])

    @pl.when(i == 0)
    def _():
        g_in.start()
        f_in.start()
        for t in (5, 0, 6, 1, 7, 2, 8, 3, 9, 4):
            load(t).start()
        g_in.wait()
        lane = lax.broadcasted_iota(jnp.int32, (FRAMES, 128), 1)
        first = CLS - LAST
        here = (lane >= first) & (lane < first + 3)
        loss[0] = jnp.sum(jnp.where(here, l0[...].astype(F32), 0.0))
        loss[1] = jnp.sum(jnp.where(here, g[:, LAST - HALF:].astype(F32), 0.0))
        f_in.wait()

    block = block_of(i)
    load(block).wait()
    rows = pl.ds(pl.multiple_of(block * 128, 128), 128)

    @pl.when(lax.rem(i, 2) == 0)
    def _():
        cols = pl.ds(pl.multiple_of(block * 128 - HALF, 128), 128)
        gradient = lax.dot_general(g[:, cols], f[...], (((0,), (0,)), ((), ())), preferred_element_type=F32)
        out[...] = wf[rows, :] - RATE * gradient

    @pl.when(lax.rem(i, 2) == 1)
    def _():
        out[...] = wf[rows, :]


def per_device(inputs, projection, offsets, labels, weights):
    vm = pl.BlockSpec(memory_space=pltpu.VMEM)
    hbm = pl.BlockSpec(memory_space=pl.ANY)
    v = pltpu.VMEM
    wide = WIDE
    f1, g1, l0, wp = pl.pallas_call(
        step_kernel,
        out_shape=(
            jax.ShapeDtypeStruct((FRAMES, FEATS), BF),
            jax.ShapeDtypeStruct((FRAMES, CPAD - HALF), BF),
            jax.ShapeDtypeStruct((FRAMES, 128), BF),
            jax.ShapeDtypeStruct((CPAD, FEATS), F32),
        ),
        in_specs=[vm, hbm, vm, vm, hbm],
        out_specs=(hbm, hbm, hbm, hbm),
        scratch_shapes=[
            v((2, FRAMES, DPAD), BF), v((DPAD, FEATS), BF), v((CLS, FEATS), F32), v((128, FEATS), F32), v((FEATS, WIDE[1]), BF),
            v((2, FRAMES, FEATS), BF), v((4, 128, WIDE[1]), F32),
            v((8, 128, WIDE[1]), F32), v((8, 128, WIDE[1]), F32),
            *[v((3, 128, w), BF) for w in wide], *[v((384, w), BF) for w in wide],
            *[v((96, w), BF) for w in wide], *[v((96, w), BF) for w in wide],
            *[v((128, w), F32) for w in wide],
            v((2, 32, CPAD), F32), v((4, 64, GRAM), BF),
            v((2, 4, 32, 128), F32), v((2, 4, 32, 128), F32), v((128, 128), F32), v((FRAMES, 128), F32),
            v((2, FRAMES, CPAD), BF),
            pltpu.SemaphoreType.DMA((SENDS,)), pltpu.SemaphoreType.DMA((RECVS,)), pltpu.SemaphoreType.DMA((6,)),
        ],
        compiler_params=pltpu.CompilerParams(collective_id=0, has_side_effects=True, vmem_limit_bytes=65 * 1000 * 1000),
        name="panels",
    )(inputs, projection, offsets.reshape(1, FEATS), labels, weights.T)
    new, loss = pl.pallas_call(
        last_kernel,
        grid=(TILES,),
        out_shape=(jax.ShapeDtypeStruct((CLS, FEATS), F32), jax.ShapeDtypeStruct((2,), F32)),
        in_specs=[hbm, hbm, hbm, pl.BlockSpec((FRAMES, 128), lambda i: (0, 0))],
        out_specs=(
            pl.BlockSpec((128, FEATS), lambda i: (block_of(i), 0)),
            pl.BlockSpec(memory_space=pltpu.SMEM),
        ),
        scratch_shapes=[
            v((CPAD, FEATS), F32), v((FRAMES, FEATS), BF), v((FRAMES, CPAD - HALF), BF),
            pltpu.SemaphoreType.DMA((2 + TILES,)),
        ],
        compiler_params=pltpu.CompilerParams(vmem_limit_bytes=62 * 2**20),
        name="last_update",
    )(wp, f1, g1, l0)
    return new.T, loss


def solution(mesh):
    return jax.shard_map(
        per_device,
        mesh=mesh,
        in_specs=(P(None, "feat", None), P(None, "feat"), P("feat"), P(), P("feat", "cls")),
        out_specs=(P("feat", "cls"), P()),
        check_vma=False,
    )
```

time: 123 us -> 113 us (0.919)
  Pallas kernels: 122 us -> 113 us
    pallas_call x1, Pallas kernels: 108 us -> 99.7 us  [per_device(): pl.pallas_call(step_kernel, out_shape=(jax.ShapeDtypeStruct((FRAMES, FEAT...]
    pallas_call x1, Pallas kernels: 14.6 us -> 12.9 us  [per_device(): pl.pallas_call(last_kernel, grid=(TILES,), out_shape=(jax.ShapeDtypeStruc...]
where the time goes in v3:
time: 113 us
  Pallas kernels  113 us (100%)
    pallas_call x1, Pallas kernels, per_device(): pl.pallas_call(step_kernel, out_shape=(jax.ShapeDtypeStruct((FRAMES, FEAT...  99.7 us
    pallas_call x1, Pallas kernels, per_device(): pl.pallas_call(last_kernel, grid=(TILES,), out_shape=(jax.ShapeDtypeStruc...  12.9 us

profile of v3, /device:TPU:1, one launch (start us, length us, event | category | flops | bytes accessed | tf_op | source)
XLA Modules:
  0.0 113.3 jit_solution(2666927899088495498)
XLA Ops:
  0.6 99.7 %panels.1 = (bf16[1024,2048]{1,0:T(8,128)(2,1)}, bf16[1024,640]{1,0:T(8,128)(2,1)}, bf16[1024,128]{1,0:T(8,128)(2,1)}, f32[1280,2048]{1,0:T(8,128)}) custom-call(bf16[2,32,360]{2,1,0:T(8,128)(2,1)} %inp.1, bf16[360,2048]{1,0:T(8,128)(2,1)} %proj.1, s32[1,2048]{1,0:T(1,128)} %bitcast.4, s32[2,1024]{1,0:T(2,128)} %lab.1, f32[1250,2048]{1,0:T(8,128)} %bitcast.3), custom_call_target="tpu_custom_call" | custom-call | tf_op jit(solution)/shard_map/panels/pallas_call | solution.py:588
  100.4 12.9 %last_update.1 = (f32[1250,2048]{1,0:T(8,128)}, f32[2]{0:T(128)}) custom-call(f32[1280,2048]{1,0:T(8,128)} %get-tuple-element.8.w_hbm, bf16[1024,2048]{1,0:T(8,128)(2,1)} %get-tuple-element.9.f_hbm, bf16[1024,640]{1,0:T(8,128)(2,1)} %get-tuple-element.10.g_hbm, bf16[1024,128]{1,0:T(8,128)(2,1)} %get-tuple-element.11.l0), custom_call_target="tpu_custom_call" | custom-call | tf_op jit(solution)/shard_map/last_update/pallas_call | solution.py:613

commit v4 on v3

--- a/solution.py
+++ b/solution.py
@@ -32,10 +32,10 @@
 
 def step_kernel(
     inp, proj, off, lab, w_hbm,
-    f1_hbm, g1_hbm, l0_hbm, wp_hbm,
-    xb, pb, wf, tail_rows, wn, fb, ows, ps, pr,
+    fb, gb, wf, tail_rows,
+    xb, pb, wn, ows, ps, pr,
     s1_0, s1_1, r1_0, r1_1, s2_0, s2_1, r2_0, r2_1, own_0, own_1,
-    so, kg, tg, ox, lt, lc, gb, ssem, rsem, lsem,
+    so, kg, tg, ox, lt, lc, ssem, rsem, lsem,
 ):
     feat, x = lax.axis_index("feat"), lax.axis_index("cls")
     c = lax.rem(feat, 2)
@@ -87,6 +87,10 @@
         start = cc * 512 + b1 * 128 + b2 * 32 + extra
         return pl.ds(pl.multiple_of(start, min(size, 128)), size)
 
+    barrier = pltpu.get_barrier_semaphore()
+    for dev in [right1, left1, across1, partner] + ring2 + others_x:
+        pl.semaphore_signal(barrier, inc=1, device_id=dev, device_id_type=MESH)
+
     w_in = pltpu.make_async_copy(w_hbm, wf, lsem.at[4])
     proj_in = pltpu.make_async_copy(proj, pb.at[pl.ds(0, DIN)], lsem.at[0])
     proj_in.start()
@@ -98,9 +102,6 @@
         xb[p, own(), :] = jnp.zeros((32, DPAD), BF)
         xb[p, own(), 0:DIN] = inp[p]
 
-    barrier = pltpu.get_barrier_semaphore()
-    for dev in [right1, left1, across1, partner] + ring2 + others_x:
-        pl.semaphore_signal(barrier, inc=1, device_id=dev, device_id_type=MESH)
     pl.semaphore_wait(barrier, 10)
 
     class Gather:
@@ -473,15 +474,11 @@
 
     lax.fori_loop(0, 8, panel_step, 0)
 
-    f1_out = pltpu.make_async_copy(fb.at[1], f1_hbm, lsem.at[1])
-    f1_out.start()
     reduce3(1)
     gg[0].step3()
     reduce5(1)
     gg[0].step4()
     gg[0].step5()
-    g0_out = pltpu.make_async_copy(gb.at[0, :, pl.ds(LAST, 128)], l0_hbm, lsem.at[4])
-    g0_out.start()
 
     tail = {
         1: [lambda: find_target(1)],
@@ -496,17 +493,11 @@
         tile = pl.ds(pl.multiple_of(t * 128, 128), 128)
         wf[tile, :] = wf[tile, :] - RATE * gradient(0, tile)
 
-        @pl.when(t >= HALF // 128)
-        def _():
-            pltpu.make_async_copy(wf.at[tile], wp_hbm.at[tile], lsem.at[2]).start()
-
         run(tail, t)
         return 0
 
     lax.fori_loop(0, TILES - 1, update_step, 0)
     tail_rows[...] = tail_rows[...] - RATE * gradient(0, pl.ds(LAST, 128))
-    wp_last = pltpu.make_async_copy(tail_rows, wp_hbm.at[pl.ds(LAST, 128)], lsem.at[5])
-    wp_last.start()
     ga.step1()
     gz.step1()
     ga.step2()
@@ -515,69 +506,48 @@
     gz.step3()
     ga.step4()
     ga.step5()
-    second = {0: [lambda: gz.step4()]}
+    second = {2: [lambda: gz.step4()]}
 
     def second_step(t, _):
         tile = pl.ds(pl.multiple_of(t * 128, 128), 128)
         run(second, t)
         wf[tile, :] = wf[tile, :] - RATE * gradient(1, tile)
-        pltpu.make_async_copy(wf.at[tile], wp_hbm.at[tile], lsem.at[2]).start()
         return 0
 
     lax.fori_loop(0, HALF // 128, second_step, 0)
     gz.step5()
-    g1_out = pltpu.make_async_copy(gb.at[1, :, pl.ds(HALF, CPAD - HALF)], g1_hbm, lsem.at[3])
-    g1_out.start()
     for fn in drain:
         fn()
-    f1_out.wait()
-    most = pl.ds(0, LAST)
-    pltpu.make_async_copy(wf.at[most], wp_hbm.at[most], lsem.at[2]).wait()
-    wp_last.wait()
-    g0_out.wait()
-    g1_out.wait()
-
-
-def block_of(i):
-    return i // 2 + 5 * (1 - lax.rem(i, 2))
-
-
-def last_kernel(w_hbm, f_hbm, g_hbm, l0, out, loss, wf, f, g, sem):
+
+
+def last_kernel(fb, gb, wf, tail_rows, out, loss):
     i = pl.program_id(0)
-    f_in = pltpu.make_async_copy(f_hbm, f, sem.at[0])
-    g_in = pltpu.make_async_copy(g_hbm, g, sem.at[1])
-
-    def load(t):
-        rows = pl.ds(pl.multiple_of(t * 128, 128), 128)
-        return pltpu.make_async_copy(w_hbm.at[rows], wf.at[rows], sem.at[2 + t])
 
     @pl.when(i == 0)
     def _():
-        g_in.start()
-        f_in.start()
-        for t in (5, 0, 6, 1, 7, 2, 8, 3, 9, 4):
-            load(t).start()
-        g_in.wait()
         lane = lax.broadcasted_iota(jnp.int32, (FRAMES, 128), 1)
         first = CLS - LAST
         here = (lane >= first) & (lane < first + 3)
-        loss[0] = jnp.sum(jnp.where(here, l0[...].astype(F32), 0.0))
-        loss[1] = jnp.sum(jnp.where(here, g[:, LAST - HALF:].astype(F32), 0.0))
-        f_in.wait()
-
-    block = block_of(i)
-    load(block).wait()
-    rows = pl.ds(pl.multiple_of(block * 128, 128), 128)
-
-    @pl.when(lax.rem(i, 2) == 0)
+        for p in range(2):
+            loss[p] = jnp.sum(jnp.where(here, gb[p, :, LAST:].astype(F32), 0.0))
+
+    cols = pl.ds(pl.multiple_of(i * 128, 128), 128)
+
+    @pl.when(i < HALF // 128)
     def _():
-        cols = pl.ds(pl.multiple_of(block * 128 - HALF, 128), 128)
-        gradient = lax.dot_general(g[:, cols], f[...], (((0,), (0,)), ((), ())), preferred_element_type=F32)
-        out[...] = wf[rows, :] - RATE * gradient
-
-    @pl.when(lax.rem(i, 2) == 1)
+        out[...] = wf[cols, :]
+
+    @pl.when(i >= HALF // 128)
     def _():
-        out[...] = wf[rows, :]
+        gradient = lax.dot_general(gb[1, :, cols], fb[1], (((0,), (0,)), ((), ())), preferred_element_type=F32)
+
+        @pl.when(i < TILES - 1)
+        def _():
+            out[...] = wf[cols, :] - RATE * gradient
+
+        @pl.when(i == TILES - 1)
+        def _():
+            out[...] = tail_rows[...] - RATE * gradient
 
 
 def per_device(inputs, projection, offsets, labels, weights):
@@ -585,47 +555,39 @@
     hbm = pl.BlockSpec(memory_space=pl.ANY)
     v = pltpu.VMEM
     wide = WIDE
-    f1, g1, l0, wp = pl.pallas_call(
+    kept = pl.pallas_call(
         step_kernel,
         out_shape=(
-            jax.ShapeDtypeStruct((FRAMES, FEATS), BF),
-            jax.ShapeDtypeStruct((FRAMES, CPAD - HALF), BF),
-            jax.ShapeDtypeStruct((FRAMES, 128), BF),
-            jax.ShapeDtypeStruct((CPAD, FEATS), F32),
+            v((2, FRAMES, FEATS), BF), v((2, FRAMES, CPAD), BF), v((CLS, FEATS), F32), v((128, FEATS), F32),
         ),
         in_specs=[vm, hbm, vm, vm, hbm],
-        out_specs=(hbm, hbm, hbm, hbm),
+        out_specs=(vm, vm, vm, vm),
         scratch_shapes=[
-            v((2, FRAMES, DPAD), BF), v((DPAD, FEATS), BF), v((CLS, FEATS), F32), v((128, FEATS), F32), v((FEATS, WIDE[1]), BF),
-            v((2, FRAMES, FEATS), BF), v((4, 128, WIDE[1]), F32),
+            v((2, FRAMES, DPAD), BF), v((DPAD, FEATS), BF), v((FEATS, WIDE[1]), BF),
+            v((4, 128, WIDE[1]), F32),
             v((8, 128, WIDE[1]), F32), v((8, 128, WIDE[1]), F32),
             *[v((3, 128, w), BF) for w in wide], *[v((384, w), BF) for w in wide],
             *[v((96, w), BF) for w in wide], *[v((96, w), BF) for w in wide],
             *[v((128, w), F32) for w in wide],
             v((2, 32, CPAD), F32), v((4, 64, GRAM), BF),
             v((2, 4, 32, 128), F32), v((2, 4, 32, 128), F32), v((128, 128), F32), v((FRAMES, 128), F32),
-            v((2, FRAMES, CPAD), BF),
             pltpu.SemaphoreType.DMA((SENDS,)), pltpu.SemaphoreType.DMA((RECVS,)), pltpu.SemaphoreType.DMA((6,)),
         ],
-        compiler_params=pltpu.CompilerParams(collective_id=0, has_side_effects=True, vmem_limit_bytes=65 * 1000 * 1000),
+        compiler_params=pltpu.CompilerParams(collective_id=0, has_side_effects=True, vmem_limit_bytes=38 * 2**20),
         name="panels",
     )(inputs, projection, offsets.reshape(1, FEATS), labels, weights.T)
     new, loss = pl.pallas_call(
         last_kernel,
         grid=(TILES,),
         out_shape=(jax.ShapeDtypeStruct((CLS, FEATS), F32), jax.ShapeDtypeStruct((2,), F32)),
-        in_specs=[hbm, hbm, hbm, pl.BlockSpec((FRAMES, 128), lambda i: (0, 0))],
+        in_specs=[vm, vm, vm, vm],
         out_specs=(
-            pl.BlockSpec((128, FEATS), lambda i: (block_of(i), 0)),
+            pl.BlockSpec((128, FEATS), lambda i: (i, 0)),
             pl.BlockSpec(memory_space=pltpu.SMEM),
         ),
-        scratch_shapes=[
-            v((CPAD, FEATS), F32), v((FRAMES, FEATS), BF), v((FRAMES, CPAD - HALF), BF),
-            pltpu.SemaphoreType.DMA((2 + TILES,)),
-        ],
-        compiler_params=pltpu.CompilerParams(vmem_limit_bytes=62 * 2**20),
+        compiler_params=pltpu.CompilerParams(vmem_limit_bytes=12 * 2**20),
         name="last_update",
-    )(wp, f1, g1, l0)
+    )(*kept)
     return new.T, loss
 
 

time: 113 us -> 107 us (0.947)
  Pallas kernels: 113 us -> 106 us
    pallas_call x1, Pallas kernels: 12.9 us -> 8.13 us  [per_device(): pl.pallas_call(last_kernel, grid=(TILES,), out_shape=(jax.ShapeDtypeStruc...]
    pallas_call x1, Pallas kernels: 99.7 us -> 98 us  [per_device(): pl.pallas_call(step_kernel, out_shape=(v((2, FRAMES, FEATS), BF), v((2, F...]
where the time goes in v4:
time: 107 us
  Pallas kernels  106 us (99%)
    pallas_call x1, Pallas kernels, per_device(): pl.pallas_call(step_kernel, out_shape=(v((2, FRAMES, FEATS), BF), v((2, F...  98 us
    pallas_call x1, Pallas kernels, per_device(): pl.pallas_call(last_kernel, grid=(TILES,), out_shape=(jax.ShapeDtypeStruc...  8.13 us

profile of v4, /device:TPU:1, one launch (start us, length us, event | category | flops | bytes accessed | tf_op | source)
XLA Modules:
  0.0 106.7 jit_solution(6617743920505079195)
XLA Ops:
  0.6 98.0 %panels.1 = (bf16[2,1024,2048]{2,1,0:T(8,128)(2,1)S(1)}, bf16[2,1024,1280]{2,1,0:T(8,128)(2,1)S(1)}, f32[1250,2048]{1,0:T(8,128)S(1)}, f32[128,2048]{1,0:T(8,128)S(1)}) custom-call(bf16[2,32,360]{2,1,0:T(8,128)(2,1)} %inp.1, bf16[360,2048]{1,0:T(8,128)(2,1)} %proj.1, s32[1,2048]{1,0:T(1,128)} %bitcast.4, s32[2,1024]{1,0:T(2,128)} %lab.1, f32[1250,2048]{1,0:T(8,128)} %bitcast.3), custom_call_target="tpu_custom_call" | custom-call | tf_op jit(solution)/shard_map/panels/pallas_call | solution.py:558
  98.6 8.1 %last_update.1 = (f32[1250,2048]{1,0:T(8,128)}, f32[2]{0:T(128)}) custom-call(bf16[2,1024,2048]{2,1,0:T(8,128)(2,1)S(1)} %get-tuple-element.8.fb, bf16[2,1024,1280]{2,1,0:T(8,128)(2,1)S(1)} %get-tuple-element.9.gb, f32[1250,2048]{1,0:T(8,128)S(1)} %get-tuple-element.10.wf, f32[128,2048]{1,0:T(8,128)S(1)} %get-tuple-element.11.tail_rows), custom_call_target="tpu_custom_call" | custom-call | tf_op jit(solution)/shard_map/last_update/pallas_call | solution.py:579
